TPU v7x, 32 devices: a whole 2x2x4 slice. The times are simulated.
32 devices in a mesh: blk: 16 (over z, y, x), grp: 2 (over core).
Axes of the slice: x: 2, y: 2, z: 4, core: 2. Of those that a mesh axis runs over, the one named last changes fastest.
Arguments:
- schur_blocks: bfloat16 [64, 1024, 1024], P(('blk', 'grp')), may hold values from -1 to 5, as said below
- residual: float32 [64, 1024, 128], P(('blk', 'grp')), may hold values from -200 to 200
- direction: float32 [64, 1024, 128], P(('blk', 'grp')), may hold values from -200 to 200
- corner_map: int32 [64, 24], P(('blk', 'grp')), may hold values from 0 to 511
- panel_order: int32 [8], replicated, may hold values from 0 to 7, each once
- coarse_factor: float32 [8, 8, 1024, 1024], P(None, None, 'blk'), may hold values from -0.0625 to 0.0625
- block_inverses: float32 [8, 1024, 1024], P(None, 'blk'), may hold values from -0.1875 to 0.1875
Outputs:
- residual_next: float32 [64, 1024, 128], P(('blk', 'grp'))
- direction_next: float32 [64, 1024, 128], P(('blk', 'grp'))
Inputs may be any that keep to these rules, and one draw needn't show every extreme that they name: `schur_blocks`: each subdomain's block is symmetric positive definite. `panel_order`: each coarse block appears once.
All inputs are finite; a program needn't handle non-finite values.
Results may differ from a plain program's by a relative error of at most 0.0048.
Values sent between devices are 32-bit elements; how exact they have to be, the bound alone decides.
No kernel may reach another device: no remote copies, remote signals or barrier semaphores. Data moves between devices by JAX's collectives and lax.ppermute only.
A program may use at most 64 MiB of HBM per device.

v0:
```python
import jax
import jax.numpy as jnp
from jax import lax
from jax.experimental import pallas as pl
from jax.experimental.pallas import tpu as pltpu
from jax.sharding import PartitionSpec as P


LANES = 128
KERNEL_VMEM = 3 << 20
BATCHES = (
    ("inv_a", 0, 2, None, None, 0),
    ("inv_b", 2, 4, None, 1, 3),
    ("inv_c", 4, 8, None, 5, 8),
    ("low_a", 0, 4, 0, 0, 1),
    ("low_b", 4, 12, 1, 2, 5),
    ("low_c", 12, 20, 1, 4, 7),
    ("low_d", 20, 28, 3, 6, 9),
)
exact = lax.Precision.HIGHEST
fine = lax.Precision.HIGH


def swap(value, mask, size):
    return lax.ppermute(value, "blk", [(i, i ^ mask) for i in range(size)])


def across(value):
    return lax.ppermute(value, "grp", [(0, 1), (1, 0)])


def after(value, other):
    return lax.optimization_barrier((value, other))[0]


def parts_over(values, masks, size):
    return [swap(value, mask, size) for value, mask in zip(values, masks)]


def total_over(value, masks, size):
    parts = parts_over([value] * len(masks), masks, size)
    total = value
    for part in parts:
        total = total + part
    return total


def times_transposed(left, right, precision):
    return lax.dot_general(
        left,
        right,
        (((1,), (1,)), ((), ())),
        precision=precision,
        preferred_element_type=jnp.float32,
    )


def put_columns_of_i(target, ref, slot, place):
    quarter = ref.shape[-1] // 4
    first = lax.broadcasted_iota(jnp.int32, (ref.shape[-2], LANES), 1) < LANES // 2
    for low in range(2):

        @pl.when(place % 2 == low)
        def _(low=low):
            for pair in range(2):
                even, odd = (
                    ref[slot, :, pl.ds(pl.multiple_of(member * quarter + place // 2 * LANES, LANES), LANES)]
                    for member in (2 * pair, 2 * pair + 1)
                )
                even, odd = (pltpu.roll(even, LANES // 2, 1), odd) if low else (even, pltpu.roll(odd, LANES // 2, 1))
                target[:, pair * LANES : (pair + 1) * LANES] = jnp.where(first, even, odd)


def put_columns_of_j(target, ref, slot, place):
    quarter = ref.shape[-1] // 4
    target[...] = ref[slot, :, pl.ds(pl.multiple_of(place * quarter, quarter), quarter)]


def pack(array, order, groups, place, core, columns, earlier):
    rows, width = array.shape[-2:]
    quarter = width // 4
    total = sum(len(group) for group in groups)
    scalars = jnp.stack([place, core]).astype(jnp.int32)
    if earlier is not None:
        scalars = after(scalars, earlier)

    def body(info, turns, source, *rest):
        outs, held, arrived = rest[:-2], rest[-2], rest[-1]
        my_place, my_core = info[0], info[1]
        copies = []
        for picks in [picks for group in groups for picks in group]:
            block = source
            for pick in picks:
                block = block.at[turns[pick]]
            slot = len(copies)
            copies.append(pltpu.make_async_copy(block, held.at[slot], arrived.at[slot]))
            copies[-1].start()

        def put(target, at, slot, whose):
            columns(target.at[at], held, slot, whose)

        slot = 0
        for number, group in enumerate(groups):
            own, near, far = outs[3 * number : 3 * number + 3]
            for at in range(len(group)):
                copies[slot].wait()
                put(own, at, slot, my_place)
                put(near, at, slot, my_place ^ (1 + my_core))

                @pl.when(my_core == at % 2)
                def _(far=far, at=at, slot=slot):
                    put(far, at // 2, slot, my_place ^ 3)

                slot += 1

    shapes = [(count, rows, quarter) for group in groups for count in (len(group), len(group), len(group) // 2)]
    outs = pl.pallas_call(
        body,
        out_shape=[jax.ShapeDtypeStruct(shape, jnp.float32) for shape in shapes],
        grid_spec=pltpu.PrefetchScalarGridSpec(
            num_scalar_prefetch=2,
            grid=(1,),
            in_specs=[pl.BlockSpec(memory_space=pltpu.HBM)],
            out_specs=[pl.BlockSpec(shape, lambda *_: (0, 0, 0)) for shape in shapes],
            scratch_shapes=[pltpu.VMEM((total, rows, width), jnp.float32), pltpu.SemaphoreType.DMA((total,))],
        ),
        cost_estimate=pl.CostEstimate(flops=0, bytes_accessed=total * rows * width * 6, transcendentals=0),
        compiler_params=pltpu.CompilerParams(vmem_limit_bytes=KERNEL_VMEM + total * rows * width * 10),
        name="pack",
    )(scalars, order, pltpu.with_memory_space_constraint(array, pltpu.HBM))
    return [outs[3 * number : 3 * number + 3] for number in range(len(groups))]


def unpack(own, near, far, place, core):
    count, rows, quarter = own.shape
    scalars = jnp.stack([place, core]).astype(jnp.int32)

    def body(info, own_ref, near_ref, near_other, far_ref, far_other, out):
        my_place, my_core = info[0], info[1]

        def put(slot, code, value):
            out[slot, pl.ds(pl.multiple_of((my_place ^ code) * rows, rows), rows), :] = value

        for slot in range(2):
            put(slot, 0, own_ref[slot])
            put(slot, 1 + my_core, near_ref[slot])
            put(slot, 2 - my_core, near_other[slot])
            put(slot, 3, jnp.where(my_core == slot, far_ref[0], far_other[0]))

    single = pl.BlockSpec((1, rows, quarter), lambda step, *_: (step, 0, 0))
    double = pl.BlockSpec((2, rows, quarter), lambda step, *_: (step, 0, 0))
    return pl.pallas_call(
        body,
        out_shape=jax.ShapeDtypeStruct((count, 4 * rows, quarter), jnp.float32),
        grid_spec=pltpu.PrefetchScalarGridSpec(
            num_scalar_prefetch=1,
            grid=(count // 2,),
            in_specs=[double, double, double, single, single],
            out_specs=pl.BlockSpec((2, 4 * rows, quarter), lambda step, *_: (step, 0, 0)),
        ),
        cost_estimate=pl.CostEstimate(flops=0, bytes_accessed=count * rows * quarter * 32, transcendentals=0),
        compiler_params=pltpu.CompilerParams(vmem_limit_bytes=KERNEL_VMEM),
        name="unpack",
    )(scalars, own, *near, *far)


def exchange(packed, masks, size, place, core):
    own, near, far = packed
    routes = [(2 * i + c, 2 * (i ^ masks[c]) + c) for i in range(size) for c in range(2)]
    near = lax.ppermute(near, ("blk", "grp"), routes)
    far = swap(far, masks[2], size)
    near_other, far_other = across(near), across(far)
    return unpack(own, (near, near_other), (far, far_other), place, core)


def grid_local(size, schur_blocks, residual, direction, corner_map, panel_order, coarse_factor, block_inverses):
    panels, rows_b, width = block_inverses.shape
    sub_count, corners = corner_map.shape
    vectors = residual.shape[-1]
    half = vectors // 2
    quarter = width // 4
    here = sub_count * corners
    device = lax.axis_index("blk")
    core = lax.axis_index("grp")
    place_i, place_j = device % 4, device // 4
    masks_i, masks_j = (1, 2, 3), (4, 8, 12)

    inverses, coupling, packed = {}, {}, {}
    pairs = [(t, u) for t in range(panels) for u in range(t)]

    def at_step(step, message):
        for kind in ("inv", "low"):
            chosen = [batch for batch in BATCHES if batch[0].startswith(kind) and batch[3] == step]
            if not chosen:
                continue
            if kind == "inv":
                groups = [[(t,) for t in range(low, high)] for _, low, high, *_ in chosen]
                how = (block_inverses, panel_order, groups, place_j, core, put_columns_of_j, message)
            else:
                groups = [pairs[low:high] for _, low, high, *_ in chosen]
                how = (coarse_factor, panel_order, groups, place_i, core, put_columns_of_i, message)
            packed.update(zip([batch[0] for batch in chosen], pack(*how)))
        for name, low, high, packing, sending, _ in BATCHES:
            if sending != step:
                continue
            ready = packed[name]
            if packing != sending:
                ready = [*ready[:1], *after(tuple(ready[1:]), message)]
            if name.startswith("inv"):
                blocks = exchange(ready, masks_j, size, place_j, core)
                inverses.update({low + at: blocks[at] for at in range(high - low)})
            else:
                blocks = exchange(ready, masks_i, size, place_i, core)
                coupling.update({pair: blocks[at] for at, pair in enumerate(pairs[low:high])})

    at_step(None, None)

    applied = jnp.einsum(
        "sij,sjv->siv", schur_blocks, direction.astype(jnp.bfloat16), preferred_element_type=jnp.float32
    )
    sums = jnp.stack(
        [
            jnp.sum(residual * residual, axis=(0, 1)),
            jnp.sum(direction * applied, axis=(0, 1)),
            jnp.sum(residual * applied, axis=(0, 1)),
            jnp.sum(applied * applied, axis=(0, 1)),
        ]
    )
    corner_res = residual[:, :corners, :].reshape(here, vectors)
    corner_app = applied[:, :corners, :].reshape(here, vectors)
    low_half = jnp.concatenate([corner_res[:, :half], corner_app[:, :half]], axis=1)
    high_half = jnp.concatenate([corner_res[:, half:], corner_app[:, half:]], axis=1)
    slots = corner_map.reshape(1, here).astype(jnp.float32)
    common = jnp.concatenate([sums, jnp.pad(slots, ((0, 3), (0, vectors - here)))], axis=0)
    keep = jnp.where(core == 0, low_half, high_half)
    give = jnp.where(core == 0, high_half, low_half)
    other = across(jnp.concatenate([give, common], axis=0))
    values = jnp.concatenate([keep, other[:here]], axis=0)
    sums = sums + other[here : here + 4]
    slots = jnp.concatenate([slots, other[here + 4 : here + 5, :here]], axis=1).astype(jnp.int32)[0]

    panel, row = slots // rows_b, slots % rows_b
    turn = jnp.sum(
        jnp.where(panel[:, None] == panel_order[None, :], jnp.arange(panels, dtype=jnp.int32)[None, :], 0), axis=1
    )
    columns = lax.broadcasted_iota(jnp.int32, (2 * here, panels * quarter), 1)
    into = (columns == (turn * quarter + place_i * rows_b + row)[:, None]).astype(jnp.float32)
    outof = (columns == (turn * quarter + place_j * rows_b + row)[:, None]).astype(jnp.float32)
    coarse = lax.dot_general(
        values, into, (((0,), (0,)), ((), ())), precision=exact, preferred_element_type=jnp.float32
    )

    pairwise = lax.broadcasted_iota(jnp.int32, (2 * here, 2 * rows_b), 1)
    into_first = (turn == 0)[:, None] & (pairwise == (place_i % 2 * rows_b + row)[:, None])
    first = lax.dot_general(
        values,
        into_first.astype(jnp.float32),
        (((0,), (0,)), ((), ())),
        precision=exact,
        preferred_element_type=jnp.float32,
    )
    first = jnp.concatenate([first, jnp.pad(sums, ((0, 4), (0, 0)))], axis=0)
    at_step(0, first)
    parts = parts_over([first] * 3, masks_i, size)
    same, other = first + parts[0], parts[1] + parts[2]
    in_low = place_i // 2 == 0
    with_sums = jnp.concatenate([jnp.where(in_low, same, other), jnp.where(in_low, other, same)], axis=1)
    sums = same[vectors:] + other[vectors:]
    partial = times_transposed(with_sums[:vectors], inverses[0], fine)
    with_sums = jnp.concatenate([partial, jnp.pad(sums, ((0, 0), (0, quarter - vectors)))], axis=0)
    at_step(1, with_sums)
    at_step("1b", with_sums)
    with_sums = total_over(with_sums, masks_j, size)
    norm_now, curvature, crossed, squared = (with_sums[vectors + k, :vectors] for k in range(4))
    step_size = norm_now / curvature
    norm_next = norm_now - step_size * (2.0 * crossed - step_size * squared)
    residual = residual - step_size * applied
    residual, moved = lax.optimization_barrier((residual, residual + norm_next / norm_now * direction))
    step_half = jnp.where(core == 0, step_size[:half], step_size[half:])[:, None]
    solved = [with_sums[:half] - step_half * with_sums[half:vectors]]
    coarse = coarse[:half] - step_half * coarse[half:]

    for t in range(1, panels):
        target = coarse[:, t * quarter : (t + 1) * quarter]
        for u in range(t - 1):
            target = target - times_transposed(solved[u], coupling[t, u], fine)
        target = lax.optimization_barrier(target)
        target = target - times_transposed(solved[t - 1], coupling[t, t - 1], fine)
        at_step(2 * t, target)
        target = total_over(target, masks_i, size)
        partial = times_transposed(target, inverses[t], fine)
        at_step(2 * t + 1, partial)
        if t + 1 < panels:
            solved.append(total_over(partial, masks_j, size))

    halves = partial[:, : 2 * rows_b], partial[:, 2 * rows_b :]
    own_low = place_j // 2 == 0
    mine, others = jnp.where(own_low, halves[0], halves[1]), jnp.where(own_low, halves[1], halves[0])
    parts = parts_over([mine, others, others], masks_j, size)
    last = mine + parts[0] + parts[1] + parts[2]
    outof_last = (turn == panels - 1)[:, None] & (pairwise == (place_j % 2 * rows_b + row)[:, None])

    correction = 0.0
    for t in range(panels - 1):
        correction = correction + times_transposed(outof[:, t * quarter : (t + 1) * quarter], solved[t], exact)
    correction = lax.optimization_barrier(correction)
    correction = correction + times_transposed(outof_last.astype(jnp.float32), last, exact)
    other = across(correction[here:])
    correction = jnp.where(
        core == 0,
        jnp.concatenate([correction[:here], other], axis=1),
        jnp.concatenate([other, correction[:here]], axis=1),
    ).reshape(sub_count, corners, vectors)
    return (residual, moved.at[:, :corners, :].add(correction))


def squares(residual):
    return lax.psum(jnp.sum(residual * residual, axis=(0, 1)), ("blk", "grp"))


def solve(coarse, panel_order, coarse_factor, block_inverses):
    panels = coarse.shape[0]
    pending = jnp.zeros_like(coarse)
    solved = jnp.zeros_like(coarse)
    for position in range(panels):
        current = panel_order[position]
        target = lax.dynamic_index_in_dim(coarse - pending, current, 0, keepdims=False)
        inverse = lax.dynamic_index_in_dim(block_inverses, current, 0, keepdims=False)
        block_value = jnp.dot(
            inverse,
            lax.all_gather(target, "blk", axis=0, tiled=True),
            precision=exact,
            preferred_element_type=jnp.float32,
        )
        solved = lax.dynamic_update_index_in_dim(solved, block_value, current, 0)
        if position + 1 < panels:
            coupling = lax.dynamic_index_in_dim(coarse_factor, current, 1, keepdims=False)
            pending = pending + jnp.einsum(
                "aic,cv->aiv", coupling, lax.all_gather(block_value, "blk", axis=0, tiled=True), precision=exact
            )
    return solved


def row_local(schur_blocks, residual, direction, corner_map, panel_order, coarse_factor, block_inverses):
    panels, rows_b = block_inverses.shape[:2]
    sub_count, corners = corner_map.shape
    columns_iota = lax.broadcasted_iota(jnp.int32, (sub_count, corners, panels * rows_b), 2)
    placing = (corner_map[:, :, None] == columns_iota).astype(jnp.float32)
    norm_now = squares(residual)
    applied = jnp.einsum(
        "sij,sjv->siv", schur_blocks, direction.astype(jnp.bfloat16), preferred_element_type=jnp.float32
    )
    curvature = lax.psum(jnp.sum(direction * applied, axis=(0, 1)), ("blk", "grp"))
    residual = residual - norm_now / curvature * applied
    norm_next = squares(residual)
    corner_part = jnp.einsum("scm,scv->mv", placing, residual[:, :corners, :], precision=exact)
    coarse_part = lax.psum(corner_part.reshape(panels, rows_b, -1), "grp")
    solved = solve(coarse_part, panel_order, coarse_factor, block_inverses)
    correction = jnp.einsum("scm,mv->scv", placing, solved.reshape(panels * rows_b, -1), precision=exact)
    direction = (residual + norm_next / norm_now * direction).at[:, :corners, :].add(correction)
    return (residual, direction)


def solution(mesh):
    in_specs = (
        P(("blk", "grp"), None, None),
        P(("blk", "grp"), None, None),
        P(("blk", "grp"), None, None),
        P(("blk", "grp"), None),
        P(),
        P(None, None, "blk", None),
        P(None, "blk", None),
    )
    out_specs = (P(("blk", "grp"), None, None), P(("blk", "grp"), None, None))
    size = mesh.shape["blk"]

    def local(*args):
        rows_b, _ = args[-1].shape[1:]
        panels, corners = args[-1].shape[0], args[3].shape[0] * args[3].shape[1]
        as_grid = (
            size == 16
            and mesh.shape["grp"] == 2
            and 2 * rows_b == LANES
            and panels % 2 == 0
            and args[1].shape[-1] == LANES
            and corners % 8 == 0
            and corners <= LANES
        )
        return grid_local(size, *args) if as_grid else row_local(*args)

    return jax.shard_map(local, mesh=mesh, in_specs=in_specs, out_specs=out_specs, check_vma=False)
```

profile of v0, /device:TPU:0, one launch (start us, length us, event | category | flops | bytes accessed | tf_op | source)
XLA Modules:
  0.0 196.8 jit_solution(505614260478330862)
XLA Ops:
  0.7 4.5 %multiply_reduce_fusion = (f32[128]{0:T(128)S(1)}, f32[128]{0:T(128)S(1)}, f32[128]{0:T(128)S(1)}, f32[128]{0:T(128)S(1)}, f32[2,1024,128]{2,1,0:T(8,128)S(1)}) fusion(f32[2,1024,128]{2,1,0:T(8,128)} %param.10, f32[2,1024,128]{2,1,0:T(8,128)} %param.11, bf16[2,1024,1024]{2,1,0:T(8,128)(2,1)} %param.9), kind=kOutput, calls=%fused_computation.31 | convolution fusion | flops 539229696 | bytes 7342080 | tf_op jit(solution)/shard_map/sij,sjv->siv/dot_general | solution.py:218
  7.1 2.1 %pack.4 = (f32[2,64,256]{2,1,0:T(8,128)S(1)}, f32[2,64,256]{2,1,0:T(8,128)S(1)}, f32[1,64,256]{2,1,0:T(8,128)S(1)}, f32[2,64,256]{2,1,0:T(8,128)S(1)}, f32[2,64,...) custom-call(s32[2]{0:T(128)S(1)} %pad_add_fusion.info, ...), custom_call_target="tpu_custom_call" | custom-call | bytes 3145728 | tf_op jit(solution)/shard_map/pack/pallas_call | solution.py:117
  10.6 2.6 %collective-permute-start.4 = (f32[2,64,256]{2,1,0:T(8,128)S(1)}, f32[2,64,256]{2,1,0:T(8,128)S(1)}, u32[]{:S(2)}, u32[]{:S(2)}) collective-permute-start(f32[2,64,256]{2,1,0:T(8,128)S(1)} %get-tuple-element.51), channel_id=1, source_target_pairs={{0,8},{1,17},{2,10},{3,19},{4,12},{5,21},{6,14},{7,23},{8,0},{9,25... | collective-permute-start | bytes 393224 | tf_op jit(solution)/shard_map/ppermute | solution.py:170
  13.2 2.5 %collective-permute-start.6 = (f32[1,64,256]{2,1,0:T(8,128)S(1)}, f32[1,64,256]{2,1,0:T(8,128)S(1)}, u32[]{:S(2)}, u32[]{:S(2)}) collective-permute-start(f32[1,64,256]{2,1,0:T(8,128)S(1)} %get-tuple-element.52), channel_id=1, source_target_pairs={{0,24},{2,26},{4,28},{6,30},{8,16},{10,18},{12,20},{14,22},{16,8},... | collective-permute-start | bytes 196616 | tf_op jit(solution)/shard_map/ppermute | solution.py:25
  21.6 2.5 %pack.5 = (f32[4,64,256]{2,1,0:T(8,128)S(1)}, f32[4,64,256]{2,1,0:T(8,128)S(1)}, f32[2,64,256]{2,1,0:T(8,128)S(1)}) custom-call(s32[2]{0:T(128)S(1)} %pad_add_fusion.1.info, s32[8]{0:T(128)S(1)} %copy-done, f32[8,8,64,1024]{3,2,1,0:T(8,128)} %source.7), custom_call_target="tpu_custom_call" | custom-call | bytes 1572864 | tf_op jit(solution)/shard_map/pack/pallas_call | solution.py:117
  31.9 2.2 %collective-permute-start.8 = (f32[136,256]{1,0:T(8,128)S(1)}, f32[136,256]{1,0:T(8,128)S(1)}, u32[]{:S(2)}, u32[]{:S(2)}) collective-permute-start(f32[136,256]{1,0:T(8,128)S(1)} %select_maximum_fusion), channel_id=1, source_target_pairs={{0,8},{2,10},{4,12},{6,14},{8,0},{10,2},{12,4},{14,6},{16,24},{18,... | collective-permute-start | bytes 417800 | tf_op jit(solution)/shard_map/ppermute | solution.py:25
  35.0 3.3 %collective-permute-done.10 = f32[136,256]{1,0:T(8,128)S(1)} collective-permute-done((f32[136,256]{1,0:T(8,128)S(1)}, f32[136,256]{1,0:T(8,128)S(1)}, u32[]{:S(2)}, u32[]{:S(2)}) %collective-permute-start.10) | collective-permute-done | bytes 139296 | tf_op jit(solution)/shard_map/ppermute | solution.py:25
  39.6 8.6 %collective-permute-done.9 = f32[136,256]{1,0:T(8,128)S(1)} collective-permute-done((f32[136,256]{1,0:T(8,128)S(1)}, f32[136,256]{1,0:T(8,128)S(1)}, u32[]{:S(2)}, u32[]{:S(2)}) %collective-permute-start.9) | collective-permute-done | bytes 139296 | tf_op jit(solution)/shard_map/ppermute | solution.py:25
  59.3 3.4 %collective-permute-start.18 = (f32[64,256]{1,0:T(8,128)S(1)}, f32[64,256]{1,0:T(8,128)S(1)}, u32[]{:S(2)}, u32[]{:S(2)}) collective-permute-start(f32[64,256]{1,0:T(8,128)S(1)} %fusion.51), channel_id=1, source_target_pairs={{0,8},{2,10},{4,12},{6,14},{8,0},{10,2},{12,4},{14,6},{16,24},{18,... | collective-permute-start | bytes 196616 | tf_op jit(solution)/shard_map/ppermute | solution.py:25
  63.0 1.8 collective-permute-done.20
  69.8 6.4 %pack.6 = (f32[8,64,256]{2,1,0:T(8,128)S(1)}, f32[8,64,256]{2,1,0:T(8,128)}, f32[4,64,256]{2,1,0:T(8,128)S(1)}, f32[8,64,256]{2,1,0:T(8,128)S(1)}, f32[8,64,256]{2,1,0:T(8,128)S(1)}, /*index=5*/f32[4,64,256]{2,1,0:T(8,128)S(1)}) custom-call(s32[2]{0:T(128)S(1)} %pad_add_fusion.1.info, s32[8]{0:T(128)S(1)} %copy-done, f32[8,8,64,1024]{3,2,1,0:T(8,128)} %source.7), custom_call_target="tpu_custom_call" | custom-call | bytes 6291456 | tf_op jit(solution)/shard_map/pack/pallas_call | solution.py:117
  78.6 2.3 %collective-permute-start.30 = (f32[64,256]{1,0:T(8,128)S(1)}, f32[64,256]{1,0:T(8,128)S(1)}, u32[]{:S(2)}, u32[]{:S(2)}) collective-permute-start(f32[64,256]{1,0:T(8,128)S(1)} %fusion.50), channel_id=1, source_target_pairs={{0,24},{2,26},{4,28},{6,30},{8,16},{10,18},{12,20},{14,22},{16,8},... | collective-permute-start | bytes 196616 | tf_op jit(solution)/shard_map/ppermute | solution.py:25
  82.7 1.8 collective-permute-start.28
  86.6 3.5 %pack.7 = (f32[8,64,256]{2,1,0:T(8,128)S(1)}, f32[8,64,256]{2,1,0:T(8,128)S(1)}, f32[4,64,256]{2,1,0:T(8,128)S(1)}) custom-call(s32[2]{0:T(128)S(1)} %pad_add_fusion.1.info, s32[8]{0:T(128)S(1)} %copy-done, f32[8,8,64,1024]{3,2,1,0:T(8,128)} %source.7), custom_call_target="tpu_custom_call" | custom-call | bytes 3145728 | tf_op jit(solution)/shard_map/pack/pallas_call | solution.py:117
  91.7 1.9 collective-permute-start.53
  95.9 4.9 %collective-permute-done.46.far_ref = f32[2,64,256]{2,1,0:T(8,128)S(1)} collective-permute-done((f32[2,64,256]{2,1,0:T(8,128)S(1)}, f32[2,64,256]{2,1,0:T(8,128)S(1)}, u32[]{:S(2)}, u32[]{:S(2)}) %collective-permute-start.46) | collective-permute-done | bytes 131104 | tf_op jit(solution)/shard_map/ppermute | solution.py:25
  118.0 2.9 %collective-permute-start.38 = (f32[64,256]{1,0:T(8,128)S(1)}, f32[64,256]{1,0:T(8,128)S(1)}, u32[]{:S(2)}, u32[]{:S(2)}) collective-permute-start(f32[64,256]{1,0:T(8,128)S(1)} %fusion.47), channel_id=1, source_target_pairs={{0,8},{2,10},{4,12},{6,14},{8,0},{10,2},{12,4},{14,6},{16,24},{18,... | collective-permute-start | bytes 196616 | tf_op jit(solution)/shard_map/ppermute | solution.py:25
  121.2 2.1 %collective-permute-done.40 = f32[64,256]{1,0:T(8,128)S(1)} collective-permute-done((f32[64,256]{1,0:T(8,128)S(1)}, f32[64,256]{1,0:T(8,128)S(1)}, u32[]{:S(2)}, u32[]{:S(2)}) %collective-permute-start.40) | collective-permute-done | bytes 65568 | tf_op jit(solution)/shard_map/ppermute | solution.py:25
  132.2 7.9 %collective-permute-done.43 = f32[64,256]{1,0:T(8,128)S(1)} collective-permute-done((f32[64,256]{1,0:T(8,128)S(1)}, f32[64,256]{1,0:T(8,128)S(1)}, u32[]{:S(2)}, u32[]{:S(2)}) %collective-permute-start.43) | collective-permute-done | bytes 65568 | tf_op jit(solution)/shard_map/ppermute | solution.py:25
  142.0 3.6 %collective-permute-start.48 = (f32[64,256]{1,0:T(8,128)S(1)}, f32[64,256]{1,0:T(8,128)S(1)}, u32[]{:S(2)}, u32[]{:S(2)}) collective-permute-start(f32[64,256]{1,0:T(8,128)S(1)} %fusion.43), channel_id=1, source_target_pairs={{0,8},{2,10},{4,12},{6,14},{8,0},{10,2},{12,4},{14,6},{16,24},{18,... | collective-permute-start | bytes 196616 | tf_op jit(solution)/shard_map/ppermute | solution.py:25
  156.0 1.8 collective-permute-start.60
  172.5 1.9 collective-permute-start.70
  175.0 2.0 %collective-permute-start.68 = (f32[64,256]{1,0:T(8,128)S(1)}, f32[64,256]{1,0:T(8,128)S(1)}, u32[]{:S(2)}, u32[]{:S(2)}) collective-permute-start(f32[64,256]{1,0:T(8,128)S(1)} %fusion.32), channel_id=1, source_target_pairs={{0,8},{2,10},{4,12},{6,14},{8,0},{10,2},{12,4},{14,6},{16,24},{18,... | collective-permute-start | bytes 196616 | tf_op jit(solution)/shard_map/ppermute | solution.py:25
  187.0 1.9 collective-permute-start.76
  (292 shorter events, 116.7 us)
Async XLA Ops:
  10.6 16.6 %collective-permute-start.4 = (f32[2,64,256]{2,1,0:T(8,128)S(1)}, f32[2,64,256]{2,1,0:T(8,128)S(1)}, u32[]{:S(2)}, u32[]{:S(2)}) collective-permute-start(f32[2,64,256]{2,1,0:T(8,128)S(1)} %get-tuple-element.51), channel_id=1, source_target_pairs={{0,8},{1,17},{2,10},{3,19},{4,12},{5,21},{6,14},{7,23},{8,0},{9,25... | collective-permute-start | bytes 393224 | tf_op jit(solution)/shard_map/ppermute | solution.py:170
  13.2 10.9 %collective-permute-start.6 = (f32[1,64,256]{2,1,0:T(8,128)S(1)}, f32[1,64,256]{2,1,0:T(8,128)S(1)}, u32[]{:S(2)}, u32[]{:S(2)}) collective-permute-start(f32[1,64,256]{2,1,0:T(8,128)S(1)} %get-tuple-element.52), channel_id=1, source_target_pairs={{0,24},{2,26},{4,28},{6,30},{8,16},{10,18},{12,20},{14,22},{16,8},... | collective-permute-start | bytes 196616 | tf_op jit(solution)/shard_map/ppermute | solution.py:25
  31.1 17.1 %collective-permute-start.9 = (f32[136,256]{1,0:T(8,128)S(1)}, f32[136,256]{1,0:T(8,128)S(1)}, u32[]{:S(2)}, u32[]{:S(2)}) collective-permute-start(f32[136,256]{1,0:T(8,128)S(1)} %select_maximum_fusion), channel_id=1, source_target_pairs={{0,16},{2,18},{4,20},{6,22},{8,24},{10,26},{12,28},{14,30},{16,0},... | collective-permute-start | bytes 417800 | tf_op jit(solution)/shard_map/ppermute | solution.py:25
  31.9 16.3 %collective-permute-start.8 = (f32[136,256]{1,0:T(8,128)S(1)}, f32[136,256]{1,0:T(8,128)S(1)}, u32[]{:S(2)}, u32[]{:S(2)}) collective-permute-start(f32[136,256]{1,0:T(8,128)S(1)} %select_maximum_fusion), channel_id=1, source_target_pairs={{0,8},{2,10},{4,12},{6,14},{8,0},{10,2},{12,4},{14,6},{16,24},{18,... | collective-permute-start | bytes 417800 | tf_op jit(solution)/shard_map/ppermute | solution.py:25
  34.8 14.3 %collective-permute-start.14 = (f32[2,64,256]{2,1,0:T(8,128)S(1)}, f32[2,64,256]{2,1,0:T(8,128)S(1)}, u32[]{:S(2)}, u32[]{:S(2)}) collective-permute-start(f32[2,64,256]{2,1,0:T(8,128)S(1)} %collective-permute-done.13.far_ref), channel_id=1, source_target_pairs={{0,1},{1,0},{2,3},{3,2},{4,5},{5,4},{6,7},{7,6},{8,9},{9,8},{10,11... | collective-permute-start | bytes 393224 | tf_op jit(solution)/shard_map/ppermute | solution.py:29
  34.9 19.3 %collective-permute-start.24 = (f32[2,64,256]{2,1,0:T(8,128)S(1)}, f32[2,64,256]{2,1,0:T(8,128)S(1)}, u32[]{:S(2)}, u32[]{:S(2)}) collective-permute-start(f32[2,64,256]{2,1,0:T(8,128)S(1)} %get-tuple-element.62), channel_id=1, source_target_pairs={{0,8},{1,17},{2,10},{3,19},{4,12},{5,21},{6,14},{7,23},{8,0},{9,25... | collective-permute-start | bytes 393224 | tf_op jit(solution)/shard_map/ppermute | solution.py:170
  38.2 16.0 %collective-permute-start.26 = (f32[1,64,256]{2,1,0:T(8,128)S(1)}, f32[1,64,256]{2,1,0:T(8,128)S(1)}, u32[]{:S(2)}, u32[]{:S(2)}) collective-permute-start(f32[1,64,256]{2,1,0:T(8,128)S(1)} %get-tuple-element.63), channel_id=1, source_target_pairs={{0,24},{2,26},{4,28},{6,30},{8,16},{10,18},{12,20},{14,22},{16,8},... | collective-permute-start | bytes 196616 | tf_op jit(solution)/shard_map/ppermute | solution.py:25
  54.2 22.8 %collective-permute-start.27 = (f32[1,64,256]{2,1,0:T(8,128)S(1)}, f32[1,64,256]{2,1,0:T(8,128)S(1)}, u32[]{:S(2)}, u32[]{:S(2)}) collective-permute-start(f32[1,64,256]{2,1,0:T(8,128)S(1)} %collective-permute-done.26.far_ref), channel_id=1, source_target_pairs={{0,1},{1,0},{2,3},{3,2},{4,5},{5,4},{6,7},{7,6},{8,9},{9,8},{10,11... | collective-permute-start | bytes 196616 | tf_op jit(solution)/shard_map/ppermute | solution.py:29
  54.2 22.8 %collective-permute-start.25 = (f32[2,64,256]{2,1,0:T(8,128)S(1)}, f32[2,64,256]{2,1,0:T(8,128)S(1)}, u32[]{:S(2)}, u32[]{:S(2)}) collective-permute-start(f32[2,64,256]{2,1,0:T(8,128)S(1)} %collective-permute-done.24.near_ref), channel_id=1, source_target_pairs={{0,1},{1,0},{2,3},{3,2},{4,5},{5,4},{6,7},{7,6},{8,9},{9,8},{10,11... | collective-permute-start | bytes 393224 | tf_op jit(solution)/shard_map/ppermute | solution.py:29
  66.2 12.1 %collective-permute-start.23 = (f32[64,256]{1,0:T(8,128)S(1)}, f32[64,256]{1,0:T(8,128)S(1)}, u32[]{:S(2)}, u32[]{:S(2)}) collective-permute-start(f32[64,256]{1,0:T(8,128)S(1)} %convolution_subtract_fusion.5), channel_id=1, source_target_pairs={{0,6},{2,4},{4,2},{6,0},{8,14},{10,12},{12,10},{14,8},{16,22},{18,... | collective-permute-start | bytes 196616 | tf_op jit(solution)/shard_map/ppermute | solution.py:25
  77.8 17.9 %collective-permute-start.31 = (f32[8,64,256]{2,1,0:T(8,128)}, f32[8,64,256]{2,1,0:T(8,128)S(1)}, u32[]{:S(2)}, u32[]{:S(2)}) collective-permute-start(f32[8,64,256]{2,1,0:T(8,128)} %get-tuple-element.68), channel_id=1, source_target_pairs={{0,2},{1,5},{2,0},{3,7},{4,6},{5,1},{6,4},{7,3},{8,10},{9,13},{10,... | collective-permute-start | bytes 1572872 | tf_op jit(solution)/shard_map/ppermute | solution.py:170
  80.9 13.2 %collective-permute-start.33 = (f32[4,64,256]{2,1,0:T(8,128)}, f32[4,64,256]{2,1,0:T(8,128)S(1)}, u32[]{:S(2)}, u32[]{:S(2)}) collective-permute-start(f32[4,64,256]{2,1,0:T(8,128)} %copy-done.6), channel_id=1, source_target_pairs={{0,6},{2,4},{4,2},{6,0},{8,14},{10,12},{12,10},{14,8},{16,22},{18,... | collective-permute-start | bytes 786440 | tf_op jit(solution)/shard_map/ppermute | solution.py:25
  84.8 16.0 %collective-permute-start.44 = (f32[4,64,256]{2,1,0:T(8,128)}, f32[4,64,256]{2,1,0:T(8,128)S(1)}, u32[]{:S(2)}, u32[]{:S(2)}) collective-permute-start(f32[4,64,256]{2,1,0:T(8,128)} %copy-done.3), channel_id=1, source_target_pairs={{0,8},{1,17},{2,10},{3,19},{4,12},{5,21},{6,14},{7,23},{8,0},{9,25... | collective-permute-start | bytes 786440 | tf_op jit(solution)/shard_map/ppermute | solution.py:170
  90.7 14.7 %collective-permute-start.51 = (f32[8,64,256]{2,1,0:T(8,128)S(1)}, f32[8,64,256]{2,1,0:T(8,128)S(1)}, u32[]{:S(2)}, u32[]{:S(2)}) collective-permute-start(f32[8,64,256]{2,1,0:T(8,128)S(1)} %copy-done.2), channel_id=1, source_target_pairs={{0,2},{1,5},{2,0},{3,7},{4,6},{5,1},{6,4},{7,3},{8,10},{9,13},{10,... | collective-permute-start | bytes 1572872 | tf_op jit(solution)/shard_map/ppermute | solution.py:170
  91.7 12.2 %collective-permute-start.53 = (f32[4,64,256]{2,1,0:T(8,128)S(1)}, f32[4,64,256]{2,1,0:T(8,128)S(1)}, u32[]{:S(2)}, u32[]{:S(2)}) collective-permute-start(f32[4,64,256]{2,1,0:T(8,128)S(1)} %copy-done.5), channel_id=1, source_target_pairs={{0,6},{2,4},{4,2},{6,0},{8,14},{10,12},{12,10},{14,8},{16,22},{18,... | collective-permute-start | bytes 786440 | tf_op jit(solution)/shard_map/ppermute | solution.py:25
  95.7 10.8 %collective-permute-start.32 = (f32[8,64,256]{2,1,0:T(8,128)S(1)}, f32[8,64,256]{2,1,0:T(8,128)S(1)}, u32[]{:S(2)}, u32[]{:S(2)}) collective-permute-start(f32[8,64,256]{2,1,0:T(8,128)S(1)} %collective-permute-done.31.near_ref), channel_id=1, source_target_pairs={{0,1},{1,0},{2,3},{3,2},{4,5},{5,4},{6,7},{7,6},{8,9},{9,8},{10,11... | collective-permute-start | bytes 1572872 | tf_op jit(solution)/shard_map/ppermute | solution.py:29
  105.3 22.4 %collective-permute-start.54 = (f32[4,64,256]{2,1,0:T(8,128)S(1)}, f32[4,64,256]{2,1,0:T(8,128)S(1)}, u32[]{:S(2)}, u32[]{:S(2)}) collective-permute-start(f32[4,64,256]{2,1,0:T(8,128)S(1)} %collective-permute-done.53.far_ref), channel_id=1, source_target_pairs={{0,1},{1,0},{2,3},{3,2},{4,5},{5,4},{6,7},{7,6},{8,9},{9,8},{10,11... | collective-permute-start | bytes 786440 | tf_op jit(solution)/shard_map/ppermute | solution.py:29
  105.5 23.7 %collective-permute-start.52 = (f32[8,64,256]{2,1,0:T(8,128)S(1)}, f32[8,64,256]{2,1,0:T(8,128)S(1)}, u32[]{:S(2)}, u32[]{:S(2)}) collective-permute-start(f32[8,64,256]{2,1,0:T(8,128)S(1)} %collective-permute-done.51.near_ref), channel_id=1, source_target_pairs={{0,1},{1,0},{2,3},{3,2},{4,5},{5,4},{6,7},{7,6},{8,9},{9,8},{10,11... | collective-permute-start | bytes 1572872 | tf_op jit(solution)/shard_map/ppermute | solution.py:29
  123.3 37.1 %collective-permute-start.61 = (f32[8,64,256]{2,1,0:T(8,128)S(1)}, f32[8,64,256]{2,1,0:T(8,128)S(1)}, u32[]{:S(2)}, u32[]{:S(2)}) collective-permute-start(f32[8,64,256]{2,1,0:T(8,128)S(1)} %get-tuple-element.84), channel_id=1, source_target_pairs={{0,2},{1,5},{2,0},{3,7},{4,6},{5,1},{6,4},{7,3},{8,10},{9,13},{10,... | collective-permute-start | bytes 1572872 | tf_op jit(solution)/shard_map/ppermute | solution.py:170
  124.4 21.5 %collective-permute-start.63 = (f32[4,64,256]{2,1,0:T(8,128)S(1)}, f32[4,64,256]{2,1,0:T(8,128)S(1)}, u32[]{:S(2)}, u32[]{:S(2)}) collective-permute-start(f32[4,64,256]{2,1,0:T(8,128)S(1)} %get-tuple-element.85), channel_id=1, source_target_pairs={{0,6},{2,4},{4,2},{6,0},{8,14},{10,12},{12,10},{14,8},{16,22},{18,... | collective-permute-start | bytes 786440 | tf_op jit(solution)/shard_map/ppermute | solution.py:25
  126.2 13.9 %collective-permute-start.43 = (f32[64,256]{1,0:T(8,128)S(1)}, f32[64,256]{1,0:T(8,128)S(1)}, u32[]{:S(2)}, u32[]{:S(2)}) collective-permute-start(f32[64,256]{1,0:T(8,128)S(1)} %sub.140), channel_id=1, source_target_pairs={{0,6},{2,4},{4,2},{6,0},{8,14},{10,12},{12,10},{14,8},{16,22},{18,... | collective-permute-start | bytes 196616 | tf_op jit(solution)/shard_map/ppermute | solution.py:25
  127.7 12.4 %collective-permute-start.42 = (f32[64,256]{1,0:T(8,128)S(1)}, f32[64,256]{1,0:T(8,128)S(1)}, u32[]{:S(2)}, u32[]{:S(2)}) collective-permute-start(f32[64,256]{1,0:T(8,128)S(1)} %sub.140), channel_id=1, source_target_pairs={{0,4},{2,6},{4,0},{6,2},{8,12},{10,14},{12,8},{14,10},{16,20},{18,... | collective-permute-start | bytes 196616 | tf_op jit(solution)/shard_map/ppermute | solution.py:25
  129.2 11.7 %collective-permute-start.41 = (f32[64,256]{1,0:T(8,128)S(1)}, f32[64,256]{1,0:T(8,128)S(1)}, u32[]{:S(2)}, u32[]{:S(2)}) collective-permute-start(f32[64,256]{1,0:T(8,128)S(1)} %sub.140), channel_id=1, source_target_pairs={{0,2},{2,0},{4,6},{6,4},{8,10},{10,8},{12,14},{14,12},{16,18},{18,... | collective-permute-start | bytes 196616 | tf_op jit(solution)/shard_map/ppermute | solution.py:25
  145.9 18.0 %collective-permute-start.64 = (f32[4,64,256]{2,1,0:T(8,128)S(1)}, f32[4,64,256]{2,1,0:T(8,128)S(1)}, u32[]{:S(2)}, u32[]{:S(2)}) collective-permute-start(f32[4,64,256]{2,1,0:T(8,128)S(1)} %collective-permute-done.63.far_ref), channel_id=1, source_target_pairs={{0,1},{1,0},{2,3},{3,2},{4,5},{5,4},{6,7},{7,6},{8,9},{9,8},{10,11... | collective-permute-start | bytes 786440 | tf_op jit(solution)/shard_map/ppermute | solution.py:29
  (81 other events, 566.5 us)
where the time goes:
time: 197 us
  starting transfers between devices  85.8 us (44%)
  waiting for transfers between devices  61.7 us (31%)
  Pallas kernels  19.3 us (10%)
  matrix products  17.1 us (9%)
  other arithmetic  6.24 us (3%)
  local copies, waits for them, and re-layouts  4.87 us (2%)
    ppermute x55, starting transfers between devices, swap(): return lax.ppermute(value, 'blk', [(i, i ^ mask) for i in range(size)])  75.7 us
    ppermute x55, waiting for transfers between devices, swap(): return lax.ppermute(value, 'blk', [(i, i ^ mask) for i in range(size)])  59 us
    pallas_call x4, Pallas kernels, pack(): pl.pallas_call(body, out_shape=[jax.ShapeDtypeStruct(shape, jnp.float32)...  14.5 us
    dot_general x44, matrix products, times_transposed(): lax.dot_general(left, right, (((1,), (1,)), ((), ())), precision=precisio...  11.7 us
    ppermute x7, starting transfers between devices, exchange(): near = lax.ppermute(near, ('blk', 'grp'), routes)  7.28 us
    pallas_call x7, Pallas kernels, unpack(): pl.pallas_call(body, out_shape=jax.ShapeDtypeStruct((count, 4 * rows, qua...  4.83 us
    dot_general x1, matrix products, grid_local(): jnp.einsum('sij,sjv->siv', schur_blocks, direction.astype(jnp.bfloat16),...  4.51 us
    unnamed x52, local copies, waits for them, and re-layouts  4.36 us
  transfers between devices with their start and end apart: 78, of which 41 were waited for; matrix products, arithmetic and copies ran while one was open for 9% of the time, Pallas kernels for 9%

commit v1 on v0

--- a/solution.py
+++ b/solution.py
@@ -230,28 +230,33 @@
     corner_app = applied[:, :corners, :].reshape(here, vectors)
     low_half = jnp.concatenate([corner_res[:, :half], corner_app[:, :half]], axis=1)
     high_half = jnp.concatenate([corner_res[:, half:], corner_app[:, half:]], axis=1)
-    slots = corner_map.reshape(1, here).astype(jnp.float32)
+    own_slots = corner_map.reshape(here)
+    turn = jnp.sum(
+        jnp.where(
+            (own_slots // rows_b)[:, None] == panel_order[None, :], jnp.arange(panels, dtype=jnp.int32)[None, :], 0
+        ),
+        axis=1,
+    )
+    slots = (turn * rows_b + own_slots % rows_b).reshape(1, here).astype(jnp.float32)
     common = jnp.concatenate([sums, jnp.pad(slots, ((0, 3), (0, vectors - here)))], axis=0)
     keep = jnp.where(core == 0, low_half, high_half)
     give = jnp.where(core == 0, high_half, low_half)
     other = across(jnp.concatenate([give, common], axis=0))
     values = jnp.concatenate([keep, other[:here]], axis=0)
     sums = sums + other[here : here + 4]
-    slots = jnp.concatenate([slots, other[here + 4 : here + 5, :here]], axis=1).astype(jnp.int32)[0]
-
-    panel, row = slots // rows_b, slots % rows_b
-    turn = jnp.sum(
-        jnp.where(panel[:, None] == panel_order[None, :], jnp.arange(panels, dtype=jnp.int32)[None, :], 0), axis=1
-    )
-    columns = lax.broadcasted_iota(jnp.int32, (2 * here, panels * quarter), 1)
-    into = (columns == (turn * quarter + place_i * rows_b + row)[:, None]).astype(jnp.float32)
-    outof = (columns == (turn * quarter + place_j * rows_b + row)[:, None]).astype(jnp.float32)
+    slots = jnp.concatenate([slots, other[here + 4 : here + 5, :here]], axis=1).astype(jnp.int32)[0][:, None]
+
+    columns = lax.broadcasted_iota(jnp.int32, (1, panels * quarter), 1)
+    column_slot = columns // quarter * rows_b + columns % rows_b
+    column_place = columns % quarter // rows_b
+    into = (slots == jnp.where(column_place == place_i, column_slot, -1)).astype(jnp.float32)
+    outof = (slots == jnp.where(column_place == place_j, column_slot, -1)).astype(jnp.float32)
     coarse = lax.dot_general(
         values, into, (((0,), (0,)), ((), ())), precision=exact, preferred_element_type=jnp.float32
     )
 
-    pairwise = lax.broadcasted_iota(jnp.int32, (2 * here, 2 * rows_b), 1)
-    into_first = (turn == 0)[:, None] & (pairwise == (place_i % 2 * rows_b + row)[:, None])
+    pairwise = lax.broadcasted_iota(jnp.int32, (1, 2 * rows_b), 1)
+    into_first = slots == jnp.where(pairwise // rows_b == place_i % 2, pairwise % rows_b, -1)
     first = lax.dot_general(
         values,
         into_first.astype(jnp.float32),
@@ -298,7 +303,8 @@
     mine, others = jnp.where(own_low, halves[0], halves[1]), jnp.where(own_low, halves[1], halves[0])
     parts = parts_over([mine, others, others], masks_j, size)
     last = mine + parts[0] + parts[1] + parts[2]
-    outof_last = (turn == panels - 1)[:, None] & (pairwise == (place_j % 2 * rows_b + row)[:, None])
+    last_slot = (panels - 1) * rows_b + pairwise % rows_b
+    outof_last = slots == jnp.where(pairwise // rows_b == place_j % 2, last_slot, -1)
 
     correction = 0.0
     for t in range(panels - 1):

time: 197 us -> 195 us (0.990)
  other arithmetic: 6.24 us -> 2.99 us
    unnamed x52 -> x18, local copies, waits for them, and re-layouts: 4.36 us -> 1.97 us
  transfers between devices with their start and end apart: 78 -> 78, of which waited for: 41 -> 40; matrix products, arithmetic and copies ran while one was open for 9% -> 8% of each run, Pallas kernels for 9% -> 9%
where the time goes in v1:
time: 195 us; the launch traced here: 194 us
  starting transfers between devices  87.3 us (45%)
  waiting for transfers between devices  62.1 us (32%)
  Pallas kernels  18.5 us (9%)
  matrix products  18 us (9%)
  local copies, waits for them, and re-layouts  3.84 us (2%)
  other arithmetic  2.99 us (2%)
    ppermute x55, starting transfers between devices, swap(): return lax.ppermute(value, 'blk', [(i, i ^ mask) for i in range(size)])  76.3 us
    ppermute x55, waiting for transfers between devices, swap(): return lax.ppermute(value, 'blk', [(i, i ^ mask) for i in range(size)])  59.2 us
    pallas_call x4, Pallas kernels, pack(): pl.pallas_call(body, out_shape=[jax.ShapeDtypeStruct(shape, jnp.float32)...  13.7 us
    dot_general x44, matrix products, times_transposed(): lax.dot_general(left, right, (((1,), (1,)), ((), ())), precision=precisio...  12.5 us
    ppermute x7, starting transfers between devices, exchange(): near = lax.ppermute(near, ('blk', 'grp'), routes)  8.18 us
    pallas_call x7, Pallas kernels, unpack(): pl.pallas_call(body, out_shape=jax.ShapeDtypeStruct((count, 4 * rows, qua...  4.83 us
    dot_general x1, matrix products, grid_local(): jnp.einsum('sij,sjv->siv', schur_blocks, direction.astype(jnp.bfloat16),...  4.52 us
  transfers between devices with their start and end apart: 78, of which 40 were waited for; matrix products, arithmetic and copies ran while one was open for 8% of the time, Pallas kernels for 9%

profile of v1, /device:TPU:0, one launch (start us, length us, event | category | flops | bytes accessed | tf_op | source)
XLA Modules:
  0.0 194.3 jit_solution(986320352184238846)
XLA Ops:
  2.2 4.5 %multiply_reduce_fusion = (f32[128]{0:T(128)S(1)}, f32[128]{0:T(128)S(1)}, f32[128]{0:T(128)S(1)}, f32[128]{0:T(128)S(1)}, f32[2,1024,128]{2,1,0:T(8,128)S(1)}) fusion(f32[2,1024,128]{2,1,0:T(8,128)} %param.10, f32[2,1024,128]{2,1,0:T(8,128)} %param.11, bf16[2,1024,1024]{2,1,0:T(8,128)(2,1)} %param.9), kind=kOutput, calls=%fused_computation.31 | convolution fusion | flops 539229696 | bytes 7342080 | tf_op jit(solution)/shard_map/sij,sjv->siv/dot_general | solution.py:218
  8.6 2.1 %pack.4 = (f32[2,64,256]{2,1,0:T(8,128)S(1)}, f32[2,64,256]{2,1,0:T(8,128)S(1)}, f32[1,64,256]{2,1,0:T(8,128)S(1)}, f32[2,64,256]{2,1,0:T(8,128)S(1)}, f32[2,64,...) custom-call(s32[2]{0:T(128)S(1)} %pad_add_fusion.info, ...), custom_call_target="tpu_custom_call" | custom-call | bytes 3145728 | tf_op jit(solution)/shard_map/pack/pallas_call | solution.py:117
  10.8 2.7 %collective-permute-start.4 = (f32[2,64,256]{2,1,0:T(8,128)S(1)}, f32[2,64,256]{2,1,0:T(8,128)S(1)}, u32[]{:S(2)}, u32[]{:S(2)}) collective-permute-start(f32[2,64,256]{2,1,0:T(8,128)S(1)} %get-tuple-element.51), channel_id=1, source_target_pairs={{0,8},{1,17},{2,10},{3,19},{4,12},{5,21},{6,14},{7,23},{8,0},{9,25... | collective-permute-start | bytes 393224 | tf_op jit(solution)/shard_map/ppermute | solution.py:170
  13.4 2.5 %collective-permute-start.6 = (f32[1,64,256]{2,1,0:T(8,128)S(1)}, f32[1,64,256]{2,1,0:T(8,128)S(1)}, u32[]{:S(2)}, u32[]{:S(2)}) collective-permute-start(f32[1,64,256]{2,1,0:T(8,128)S(1)} %get-tuple-element.52), channel_id=1, source_target_pairs={{0,24},{2,26},{4,28},{6,30},{8,16},{10,18},{12,20},{14,22},{16,8},... | collective-permute-start | bytes 196616 | tf_op jit(solution)/shard_map/ppermute | solution.py:25
  20.0 2.5 %pack.5 = (f32[4,64,256]{2,1,0:T(8,128)S(1)}, f32[4,64,256]{2,1,0:T(8,128)S(1)}, f32[2,64,256]{2,1,0:T(8,128)S(1)}) custom-call(s32[2]{0:T(128)S(1)} %pad_add_fusion.1.info, s32[8]{0:T(128)S(1)} %copy-done, f32[8,8,64,1024]{3,2,1,0:T(8,128)} %source.7), custom_call_target="tpu_custom_call" | custom-call | bytes 1572864 | tf_op jit(solution)/shard_map/pack/pallas_call | solution.py:117
  30.3 2.2 %collective-permute-start.8 = (f32[136,256]{1,0:T(8,128)S(1)}, f32[136,256]{1,0:T(8,128)S(1)}, u32[]{:S(2)}, u32[]{:S(2)}) collective-permute-start(f32[136,256]{1,0:T(8,128)S(1)} %select_maximum_fusion), channel_id=1, source_target_pairs={{0,8},{2,10},{4,12},{6,14},{8,0},{10,2},{12,4},{14,6},{16,24},{18,... | collective-permute-start | bytes 417800 | tf_op jit(solution)/shard_map/ppermute | solution.py:25
  33.4 3.3 %collective-permute-done.10 = f32[136,256]{1,0:T(8,128)S(1)} collective-permute-done((f32[136,256]{1,0:T(8,128)S(1)}, f32[136,256]{1,0:T(8,128)S(1)}, u32[]{:S(2)}, u32[]{:S(2)}) %collective-permute-start.10) | collective-permute-done | bytes 139296 | tf_op jit(solution)/shard_map/ppermute | solution.py:25
  38.0 8.6 %collective-permute-done.9 = f32[136,256]{1,0:T(8,128)S(1)} collective-permute-done((f32[136,256]{1,0:T(8,128)S(1)}, f32[136,256]{1,0:T(8,128)S(1)}, u32[]{:S(2)}, u32[]{:S(2)}) %collective-permute-start.9) | collective-permute-done | bytes 139296 | tf_op jit(solution)/shard_map/ppermute | solution.py:25
  59.1 3.0 %collective-permute-start.18 = (f32[64,256]{1,0:T(8,128)S(1)}, f32[64,256]{1,0:T(8,128)S(1)}, u32[]{:S(2)}, u32[]{:S(2)}) collective-permute-start(f32[64,256]{1,0:T(8,128)S(1)} %fusion.53), channel_id=1, source_target_pairs={{0,8},{2,10},{4,12},{6,14},{8,0},{10,2},{12,4},{14,6},{16,24},{18,... | collective-permute-start | bytes 196616 | tf_op jit(solution)/shard_map/ppermute | solution.py:25
  62.3 2.0 %collective-permute-done.20 = f32[64,256]{1,0:T(8,128)S(1)} collective-permute-done((f32[64,256]{1,0:T(8,128)S(1)}, f32[64,256]{1,0:T(8,128)S(1)}, u32[]{:S(2)}, u32[]{:S(2)}) %collective-permute-start.20) | collective-permute-done | bytes 65568 | tf_op jit(solution)/shard_map/ppermute | solution.py:25
  69.3 5.6 %pack.6 = (f32[8,64,256]{2,1,0:T(8,128)S(1)}, f32[8,64,256]{2,1,0:T(8,128)S(1)}, f32[4,64,256]{2,1,0:T(8,128)S(1)}, f32[8,64,256]{2,1,0:T(8,128)S(1)}, f32[8,64,...) custom-call(s32[2]{0:T(128)S(1)} %pad_add_fusion.1.info, s32[8]{0:T(128)S(1)} %copy-done, f32[8,8,64,1024]{3,2,1,0:T(8,128)} %source.7), custom_call_target="tpu_custom_call" | custom-call | bytes 6291456 | tf_op jit(solution)/shard_map/pack/pallas_call | solution.py:117
  76.3 2.4 %collective-permute-start.30 = (f32[64,256]{1,0:T(8,128)S(1)}, f32[64,256]{1,0:T(8,128)S(1)}, u32[]{:S(2)}, u32[]{:S(2)}) collective-permute-start(f32[64,256]{1,0:T(8,128)S(1)} %fusion.52), channel_id=1, source_target_pairs={{0,24},{2,26},{4,28},{6,30},{8,16},{10,18},{12,20},{14,22},{16,8},... | collective-permute-start | bytes 196616 | tf_op jit(solution)/shard_map/ppermute | solution.py:25
  80.3 1.9 collective-permute-start.28
  83.7 3.5 %pack.7 = (f32[8,64,256]{2,1,0:T(8,128)S(1)}, f32[8,64,256]{2,1,0:T(8,128)S(1)}, f32[4,64,256]{2,1,0:T(8,128)S(1)}) custom-call(s32[2]{0:T(128)S(1)} %pad_add_fusion.1.info, s32[8]{0:T(128)S(1)} %copy-done, f32[8,8,64,1024]{3,2,1,0:T(8,128)} %source.7), custom_call_target="tpu_custom_call" | custom-call | bytes 3145728 | tf_op jit(solution)/shard_map/pack/pallas_call | solution.py:117
  91.7 2.4 %collective-permute-start.46 = (f32[2,64,256]{2,1,0:T(8,128)S(1)}, f32[2,64,256]{2,1,0:T(8,128)S(1)}, u32[]{:S(2)}, u32[]{:S(2)}) collective-permute-start(f32[2,64,256]{2,1,0:T(8,128)S(1)} %get-tuple-element.74), channel_id=1, source_target_pairs={{0,24},{2,26},{4,28},{6,30},{8,16},{10,18},{12,20},{14,22},{16,8},... | collective-permute-start | bytes 393224 | tf_op jit(solution)/shard_map/ppermute | solution.py:25
  94.3 4.1 %collective-permute-done.46.far_ref = f32[2,64,256]{2,1,0:T(8,128)S(1)} collective-permute-done((f32[2,64,256]{2,1,0:T(8,128)S(1)}, f32[2,64,256]{2,1,0:T(8,128)S(1)}, u32[]{:S(2)}, u32[]{:S(2)}) %collective-permute-start.46) | collective-permute-done | bytes 131104 | tf_op jit(solution)/shard_map/ppermute | solution.py:25
  99.0 2.5 %collective-permute-done.53.far_ref = f32[4,64,256]{2,1,0:T(8,128)S(1)} collective-permute-done((f32[4,64,256]{2,1,0:T(8,128)S(1)}, f32[4,64,256]{2,1,0:T(8,128)S(1)}, u32[]{:S(2)}, u32[]{:S(2)}) %collective-permute-start.53) | collective-permute-done | bytes 262176 | tf_op jit(solution)/shard_map/ppermute | solution.py:25
  115.9 2.7 %collective-permute-start.38 = (f32[64,256]{1,0:T(8,128)S(1)}, f32[64,256]{1,0:T(8,128)S(1)}, u32[]{:S(2)}, u32[]{:S(2)}) collective-permute-start(f32[64,256]{1,0:T(8,128)S(1)} %fusion.49), channel_id=1, source_target_pairs={{0,8},{2,10},{4,12},{6,14},{8,0},{10,2},{12,4},{14,6},{16,24},{18,... | collective-permute-start | bytes 196616 | tf_op jit(solution)/shard_map/ppermute | solution.py:25
  129.6 7.4 %collective-permute-done.43 = f32[64,256]{1,0:T(8,128)S(1)} collective-permute-done((f32[64,256]{1,0:T(8,128)S(1)}, f32[64,256]{1,0:T(8,128)S(1)}, u32[]{:S(2)}, u32[]{:S(2)}) %collective-permute-start.43) | collective-permute-done | bytes 65568 | tf_op jit(solution)/shard_map/ppermute | solution.py:25
  138.5 1.9 collective-permute-start.50
  140.4 2.6 %collective-permute-start.48 = (f32[64,256]{1,0:T(8,128)S(1)}, f32[64,256]{1,0:T(8,128)S(1)}, u32[]{:S(2)}, u32[]{:S(2)}) collective-permute-start(f32[64,256]{1,0:T(8,128)S(1)} %fusion.45), channel_id=1, source_target_pairs={{0,8},{2,10},{4,12},{6,14},{8,0},{10,2},{12,4},{14,6},{16,24},{18,... | collective-permute-start | bytes 196616 | tf_op jit(solution)/shard_map/ppermute | solution.py:25
  153.3 2.2 %collective-permute-start.60 = (f32[64,256]{1,0:T(8,128)S(1)}, f32[64,256]{1,0:T(8,128)S(1)}, u32[]{:S(2)}, u32[]{:S(2)}) collective-permute-start(f32[64,256]{1,0:T(8,128)S(1)} %fusion.40), channel_id=1, source_target_pairs={{0,24},{2,26},{4,28},{6,30},{8,16},{10,18},{12,20},{14,22},{16,8},... | collective-permute-start | bytes 196616 | tf_op jit(solution)/shard_map/ppermute | solution.py:25
  169.9 1.9 collective-permute-start.70
  184.5 2.1 %collective-permute-start.76 = (f32[64,128]{1,0:T(8,128)S(1)}, f32[64,128]{1,0:T(8,128)S(1)}, u32[]{:S(2)}, u32[]{:S(2)}) collective-permute-start(f32[64,128]{1,0:T(8,128)S(1)} %get-tuple-element.100), channel_id=1, source_target_pairs={{0,24},{2,26},{4,28},{6,30},{8,16},{10,18},{12,20},{14,22},{16,8},... | collective-permute-start | bytes 98312 | tf_op jit(solution)/shard_map/ppermute | solution.py:25
  (261 shorter events, 116.3 us)
Async XLA Ops:
  10.8 14.9 %collective-permute-start.4 = (f32[2,64,256]{2,1,0:T(8,128)S(1)}, f32[2,64,256]{2,1,0:T(8,128)S(1)}, u32[]{:S(2)}, u32[]{:S(2)}) collective-permute-start(f32[2,64,256]{2,1,0:T(8,128)S(1)} %get-tuple-element.51), channel_id=1, source_target_pairs={{0,8},{1,17},{2,10},{3,19},{4,12},{5,21},{6,14},{7,23},{8,0},{9,25... | collective-permute-start | bytes 393224 | tf_op jit(solution)/shard_map/ppermute | solution.py:170
  22.5 10.8 %collective-permute-start.11 = (f32[4,64,256]{2,1,0:T(8,128)S(1)}, f32[4,64,256]{2,1,0:T(8,128)S(1)}, u32[]{:S(2)}, u32[]{:S(2)}) collective-permute-start(f32[4,64,256]{2,1,0:T(8,128)S(1)} %get-tuple-element.57), channel_id=1, source_target_pairs={{0,2},{1,5},{2,0},{3,7},{4,6},{5,1},{6,4},{7,3},{8,10},{9,13},{10,... | collective-permute-start | bytes 786440 | tf_op jit(solution)/shard_map/ppermute | solution.py:170
  29.5 17.1 %collective-permute-start.9 = (f32[136,256]{1,0:T(8,128)S(1)}, f32[136,256]{1,0:T(8,128)S(1)}, u32[]{:S(2)}, u32[]{:S(2)}) collective-permute-start(f32[136,256]{1,0:T(8,128)S(1)} %select_maximum_fusion), channel_id=1, source_target_pairs={{0,16},{2,18},{4,20},{6,22},{8,24},{10,26},{12,28},{14,30},{16,0},... | collective-permute-start | bytes 417800 | tf_op jit(solution)/shard_map/ppermute | solution.py:25
  30.3 16.3 %collective-permute-start.8 = (f32[136,256]{1,0:T(8,128)S(1)}, f32[136,256]{1,0:T(8,128)S(1)}, u32[]{:S(2)}, u32[]{:S(2)}) collective-permute-start(f32[136,256]{1,0:T(8,128)S(1)} %select_maximum_fusion), channel_id=1, source_target_pairs={{0,8},{2,10},{4,12},{6,14},{8,0},{10,2},{12,4},{14,6},{16,24},{18,... | collective-permute-start | bytes 417800 | tf_op jit(solution)/shard_map/ppermute | solution.py:25
  33.2 14.2 %collective-permute-start.14 = (f32[2,64,256]{2,1,0:T(8,128)S(1)}, f32[2,64,256]{2,1,0:T(8,128)S(1)}, u32[]{:S(2)}, u32[]{:S(2)}) collective-permute-start(f32[2,64,256]{2,1,0:T(8,128)S(1)} %collective-permute-done.13.far_ref), channel_id=1, source_target_pairs={{0,1},{1,0},{2,3},{3,2},{4,5},{5,4},{6,7},{7,6},{8,9},{9,8},{10,11... | collective-permute-start | bytes 393224 | tf_op jit(solution)/shard_map/ppermute | solution.py:29
  33.3 19.3 %collective-permute-start.24 = (f32[2,64,256]{2,1,0:T(8,128)S(1)}, f32[2,64,256]{2,1,0:T(8,128)S(1)}, u32[]{:S(2)}, u32[]{:S(2)}) collective-permute-start(f32[2,64,256]{2,1,0:T(8,128)S(1)} %get-tuple-element.62), channel_id=1, source_target_pairs={{0,8},{1,17},{2,10},{3,19},{4,12},{5,21},{6,14},{7,23},{8,0},{9,25... | collective-permute-start | bytes 393224 | tf_op jit(solution)/shard_map/ppermute | solution.py:170
  36.7 16.0 %collective-permute-start.26 = (f32[1,64,256]{2,1,0:T(8,128)S(1)}, f32[1,64,256]{2,1,0:T(8,128)S(1)}, u32[]{:S(2)}, u32[]{:S(2)}) collective-permute-start(f32[1,64,256]{2,1,0:T(8,128)S(1)} %get-tuple-element.63), channel_id=1, source_target_pairs={{0,24},{2,26},{4,28},{6,30},{8,16},{10,18},{12,20},{14,22},{16,8},... | collective-permute-start | bytes 196616 | tf_op jit(solution)/shard_map/ppermute | solution.py:25
  52.6 22.3 %collective-permute-start.27 = (f32[1,64,256]{2,1,0:T(8,128)S(1)}, f32[1,64,256]{2,1,0:T(8,128)S(1)}, u32[]{:S(2)}, u32[]{:S(2)}) collective-permute-start(f32[1,64,256]{2,1,0:T(8,128)S(1)} %collective-permute-done.26.far_ref), channel_id=1, source_target_pairs={{0,1},{1,0},{2,3},{3,2},{4,5},{5,4},{6,7},{7,6},{8,9},{9,8},{10,11... | collective-permute-start | bytes 196616 | tf_op jit(solution)/shard_map/ppermute | solution.py:29
  52.7 22.3 %collective-permute-start.25 = (f32[2,64,256]{2,1,0:T(8,128)S(1)}, f32[2,64,256]{2,1,0:T(8,128)S(1)}, u32[]{:S(2)}, u32[]{:S(2)}) collective-permute-start(f32[2,64,256]{2,1,0:T(8,128)S(1)} %collective-permute-done.24.near_ref), channel_id=1, source_target_pairs={{0,1},{1,0},{2,3},{3,2},{4,5},{5,4},{6,7},{7,6},{8,9},{9,8},{10,11... | collective-permute-start | bytes 393224 | tf_op jit(solution)/shard_map/ppermute | solution.py:29
  65.7 10.3 %collective-permute-start.23 = (f32[64,256]{1,0:T(8,128)S(1)}, f32[64,256]{1,0:T(8,128)S(1)}, u32[]{:S(2)}, u32[]{:S(2)}) collective-permute-start(f32[64,256]{1,0:T(8,128)S(1)} %convolution_subtract_fusion.5), channel_id=1, source_target_pairs={{0,6},{2,4},{4,2},{6,0},{8,14},{10,12},{12,10},{14,8},{16,22},{18,... | collective-permute-start | bytes 196616 | tf_op jit(solution)/shard_map/ppermute | solution.py:25
  75.5 18.6 %collective-permute-start.31 = (f32[8,64,256]{2,1,0:T(8,128)S(1)}, f32[8,64,256]{2,1,0:T(8,128)S(1)}, u32[]{:S(2)}, u32[]{:S(2)}) collective-permute-start(f32[8,64,256]{2,1,0:T(8,128)S(1)} %get-tuple-element.68), channel_id=1, source_target_pairs={{0,2},{1,5},{2,0},{3,7},{4,6},{5,1},{6,4},{7,3},{8,10},{9,13},{10,... | collective-permute-start | bytes 1572872 | tf_op jit(solution)/shard_map/ppermute | solution.py:170
  78.7 13.0 %collective-permute-start.33 = (f32[4,64,256]{2,1,0:T(8,128)S(1)}, f32[4,64,256]{2,1,0:T(8,128)S(1)}, u32[]{:S(2)}, u32[]{:S(2)}) collective-permute-start(f32[4,64,256]{2,1,0:T(8,128)S(1)} %get-tuple-element.69), channel_id=1, source_target_pairs={{0,6},{2,4},{4,2},{6,0},{8,14},{10,12},{12,10},{14,8},{16,22},{18,... | collective-permute-start | bytes 786440 | tf_op jit(solution)/shard_map/ppermute | solution.py:25
  82.5 16.0 %collective-permute-start.44 = (f32[4,64,256]{2,1,0:T(8,128)S(1)}, f32[4,64,256]{2,1,0:T(8,128)S(1)}, u32[]{:S(2)}, u32[]{:S(2)}) collective-permute-start(f32[4,64,256]{2,1,0:T(8,128)S(1)} %get-tuple-element.73), channel_id=1, source_target_pairs={{0,8},{1,17},{2,10},{3,19},{4,12},{5,21},{6,14},{7,23},{8,0},{9,25... | collective-permute-start | bytes 786440 | tf_op jit(solution)/shard_map/ppermute | solution.py:170
  88.3 14.7 %collective-permute-start.51 = (f32[8,64,256]{2,1,0:T(8,128)S(1)}, f32[8,64,256]{2,1,0:T(8,128)S(1)}, u32[]{:S(2)}, u32[]{:S(2)}) collective-permute-start(f32[8,64,256]{2,1,0:T(8,128)S(1)} %get-tuple-element.78), channel_id=1, source_target_pairs={{0,2},{1,5},{2,0},{3,7},{4,6},{5,1},{6,4},{7,3},{8,10},{9,13},{10,... | collective-permute-start | bytes 1572872 | tf_op jit(solution)/shard_map/ppermute | solution.py:170
  89.8 11.7 %collective-permute-start.53 = (f32[4,64,256]{2,1,0:T(8,128)S(1)}, f32[4,64,256]{2,1,0:T(8,128)S(1)}, u32[]{:S(2)}, u32[]{:S(2)}) collective-permute-start(f32[4,64,256]{2,1,0:T(8,128)S(1)} %get-tuple-element.79), channel_id=1, source_target_pairs={{0,6},{2,4},{4,2},{6,0},{8,14},{10,12},{12,10},{14,8},{16,22},{18,... | collective-permute-start | bytes 786440 | tf_op jit(solution)/shard_map/ppermute | solution.py:25
  94.1 9.9 %collective-permute-start.32 = (f32[8,64,256]{2,1,0:T(8,128)S(1)}, f32[8,64,256]{2,1,0:T(8,128)S(1)}, u32[]{:S(2)}, u32[]{:S(2)}) collective-permute-start(f32[8,64,256]{2,1,0:T(8,128)S(1)} %collective-permute-done.31.near_ref), channel_id=1, source_target_pairs={{0,1},{1,0},{2,3},{3,2},{4,5},{5,4},{6,7},{7,6},{8,9},{9,8},{10,11... | collective-permute-start | bytes 1572872 | tf_op jit(solution)/shard_map/ppermute | solution.py:29
  102.8 22.4 %collective-permute-start.54 = (f32[4,64,256]{2,1,0:T(8,128)S(1)}, f32[4,64,256]{2,1,0:T(8,128)S(1)}, u32[]{:S(2)}, u32[]{:S(2)}) collective-permute-start(f32[4,64,256]{2,1,0:T(8,128)S(1)} %collective-permute-done.53.far_ref), channel_id=1, source_target_pairs={{0,1},{1,0},{2,3},{3,2},{4,5},{5,4},{6,7},{7,6},{8,9},{9,8},{10,11... | collective-permute-start | bytes 786440 | tf_op jit(solution)/shard_map/ppermute | solution.py:29
  103.0 23.7 %collective-permute-start.52 = (f32[8,64,256]{2,1,0:T(8,128)S(1)}, f32[8,64,256]{2,1,0:T(8,128)S(1)}, u32[]{:S(2)}, u32[]{:S(2)}) collective-permute-start(f32[8,64,256]{2,1,0:T(8,128)S(1)} %collective-permute-done.51.near_ref), channel_id=1, source_target_pairs={{0,1},{1,0},{2,3},{3,2},{4,5},{5,4},{6,7},{7,6},{8,9},{9,8},{10,11... | collective-permute-start | bytes 1572872 | tf_op jit(solution)/shard_map/ppermute | solution.py:29
  120.6 37.1 %collective-permute-start.61 = (f32[8,64,256]{2,1,0:T(8,128)S(1)}, f32[8,64,256]{2,1,0:T(8,128)S(1)}, u32[]{:S(2)}, u32[]{:S(2)}) collective-permute-start(f32[8,64,256]{2,1,0:T(8,128)S(1)} %get-tuple-element.84), channel_id=1, source_target_pairs={{0,2},{1,5},{2,0},{3,7},{4,6},{5,1},{6,4},{7,3},{8,10},{9,13},{10,... | collective-permute-start | bytes 1572872 | tf_op jit(solution)/shard_map/ppermute | solution.py:170
  121.9 21.3 %collective-permute-start.63 = (f32[4,64,256]{2,1,0:T(8,128)S(1)}, f32[4,64,256]{2,1,0:T(8,128)S(1)}, u32[]{:S(2)}, u32[]{:S(2)}) collective-permute-start(f32[4,64,256]{2,1,0:T(8,128)S(1)} %get-tuple-element.85), channel_id=1, source_target_pairs={{0,6},{2,4},{4,2},{6,0},{8,14},{10,12},{12,10},{14,8},{16,22},{18,... | collective-permute-start | bytes 786440 | tf_op jit(solution)/shard_map/ppermute | solution.py:25
  123.6 13.5 %collective-permute-start.43 = (f32[64,256]{1,0:T(8,128)S(1)}, f32[64,256]{1,0:T(8,128)S(1)}, u32[]{:S(2)}, u32[]{:S(2)}) collective-permute-start(f32[64,256]{1,0:T(8,128)S(1)} %sub.167), channel_id=1, source_target_pairs={{0,6},{2,4},{4,2},{6,0},{8,14},{10,12},{12,10},{14,8},{16,22},{18,... | collective-permute-start | bytes 196616 | tf_op jit(solution)/shard_map/ppermute | solution.py:25
  125.2 11.8 %collective-permute-start.42 = (f32[64,256]{1,0:T(8,128)S(1)}, f32[64,256]{1,0:T(8,128)S(1)}, u32[]{:S(2)}, u32[]{:S(2)}) collective-permute-start(f32[64,256]{1,0:T(8,128)S(1)} %sub.167), channel_id=1, source_target_pairs={{0,4},{2,6},{4,0},{6,2},{8,12},{10,14},{12,8},{14,10},{16,20},{18,... | collective-permute-start | bytes 196616 | tf_op jit(solution)/shard_map/ppermute | solution.py:25
  126.7 11.5 %collective-permute-start.41 = (f32[64,256]{1,0:T(8,128)S(1)}, f32[64,256]{1,0:T(8,128)S(1)}, u32[]{:S(2)}, u32[]{:S(2)}) collective-permute-start(f32[64,256]{1,0:T(8,128)S(1)} %sub.167), channel_id=1, source_target_pairs={{0,2},{2,0},{4,6},{6,4},{8,10},{10,8},{12,14},{14,12},{16,18},{18,... | collective-permute-start | bytes 196616 | tf_op jit(solution)/shard_map/ppermute | solution.py:25
  143.2 18.1 %collective-permute-start.64 = (f32[4,64,256]{2,1,0:T(8,128)S(1)}, f32[4,64,256]{2,1,0:T(8,128)S(1)}, u32[]{:S(2)}, u32[]{:S(2)}) collective-permute-start(f32[4,64,256]{2,1,0:T(8,128)S(1)} %collective-permute-done.63.far_ref), channel_id=1, source_target_pairs={{0,1},{1,0},{2,3},{3,2},{4,5},{5,4},{6,7},{7,6},{8,9},{9,8},{10,11... | collective-permute-start | bytes 786440 | tf_op jit(solution)/shard_map/ppermute | solution.py:29
  (64 other events, 439.1 us)

commit v2 on v1

--- a/solution.py
+++ b/solution.py
@@ -10,11 +10,11 @@
 KERNEL_VMEM = 3 << 20
 BATCHES = (
     ("inv_a", 0, 2, None, None, 0),
-    ("inv_b", 2, 4, None, 1, 3),
-    ("inv_c", 4, 8, None, 5, 8),
+    ("inv_b", 2, 4, 1, 1, 3),
+    ("inv_c", 4, 8, 1, 5, 8),
     ("low_a", 0, 4, 0, 0, 1),
     ("low_b", 4, 12, 1, 2, 5),
-    ("low_c", 12, 20, 1, 4, 7),
+    ("low_c", 12, 20, 2, 4, 7),
     ("low_d", 20, 28, 3, 6, 9),
 )
 exact = lax.Precision.HIGHEST

time: 195 us -> 194 us (level)
  Pallas kernels: 18.5 us -> 21.5 us
  waiting for transfers between devices: 62.1 us -> 59.4 us
    pallas_call x4 -> x6, Pallas kernels: 13.7 us -> 16.6 us  [pack(): pl.pallas_call(body, out_shape=[jax.ShapeDtypeStruct(shape, jnp.float32)...]
    ppermute x55, waiting for transfers between devices: 59.2 us -> 56.6 us  [swap(): return lax.ppermute(value, 'blk', [(i, i ^ mask) for i in range(size)])]
  transfers between devices with their start and end apart: 78 -> 78, of which waited for: 40 -> 36; matrix products, arithmetic and copies ran while one was open for 8% -> 8% of each run, Pallas kernels for 9% -> 11%
where the time goes in v2:
time: 194 us
  starting transfers between devices  86.5 us (45%)
  waiting for transfers between devices  59.4 us (31%)
  Pallas kernels  21.5 us (11%)
  matrix products  18 us (9%)
  local copies, waits for them, and re-layouts  3.84 us (2%)
  other arithmetic  2.99 us (2%)
    ppermute x55, starting transfers between devices, swap(): return lax.ppermute(value, 'blk', [(i, i ^ mask) for i in range(size)])  74.8 us
    ppermute x55, waiting for transfers between devices, swap(): return lax.ppermute(value, 'blk', [(i, i ^ mask) for i in range(size)])  56.6 us
    pallas_call x6, Pallas kernels, pack(): pl.pallas_call(body, out_shape=[jax.ShapeDtypeStruct(shape, jnp.float32)...  16.6 us
    dot_general x44, matrix products, times_transposed(): lax.dot_general(left, right, (((1,), (1,)), ((), ())), precision=precisio...  12.5 us
    ppermute x7, starting transfers between devices, exchange(): near = lax.ppermute(near, ('blk', 'grp'), routes)  8.87 us
    pallas_call x7, Pallas kernels, unpack(): pl.pallas_call(body, out_shape=jax.ShapeDtypeStruct((count, 4 * rows, qua...  4.83 us
    dot_general x1, matrix products, grid_local(): jnp.einsum('sij,sjv->siv', schur_blocks, direction.astype(jnp.bfloat16),...  4.52 us
  transfers between devices with their start and end apart: 78, of which 36 were waited for; matrix products, arithmetic and copies ran while one was open for 8% of the time, Pallas kernels for 11%

profile of v2, /device:TPU:0, one launch (start us, length us, event | category | flops | bytes accessed | tf_op | source)
XLA Modules:
  0.0 193.8 jit_solution(8889165742650586835)
XLA Ops:
  2.2 4.5 %multiply_reduce_fusion = (f32[128]{0:T(128)S(1)}, f32[128]{0:T(128)S(1)}, f32[128]{0:T(128)S(1)}, f32[128]{0:T(128)S(1)}, f32[2,1024,128]{2,1,0:T(8,128)S(1)}) fusion(f32[2,1024,128]{2,1,0:T(8,128)} %param.10, f32[2,1024,128]{2,1,0:T(8,128)} %param.11, bf16[2,1024,1024]{2,1,0:T(8,128)(2,1)} %param.9), kind=kOutput, calls=%fused_computation.31 | convolution fusion | flops 539229696 | bytes 7342080 | tf_op jit(solution)/shard_map/sij,sjv->siv/dot_general | solution.py:218
  10.2 2.7 %collective-permute-start.4 = (f32[2,64,256]{2,1,0:T(8,128)S(1)}, f32[2,64,256]{2,1,0:T(8,128)S(1)}, u32[]{:S(2)}, u32[]{:S(2)}) collective-permute-start(f32[2,64,256]{2,1,0:T(8,128)S(1)} %get-tuple-element.51), channel_id=1, source_target_pairs={{0,8},{1,17},{2,10},{3,19},{4,12},{5,21},{6,14},{7,23},{8,0},{9,25... | collective-permute-start | bytes 393224 | tf_op jit(solution)/shard_map/ppermute | solution.py:170
  12.9 2.5 %collective-permute-start.6 = (f32[1,64,256]{2,1,0:T(8,128)S(1)}, f32[1,64,256]{2,1,0:T(8,128)S(1)}, u32[]{:S(2)}, u32[]{:S(2)}) collective-permute-start(f32[1,64,256]{2,1,0:T(8,128)S(1)} %get-tuple-element.52), channel_id=1, source_target_pairs={{0,24},{2,26},{4,28},{6,30},{8,16},{10,18},{12,20},{14,22},{16,8},... | collective-permute-start | bytes 196616 | tf_op jit(solution)/shard_map/ppermute | solution.py:25
  19.5 2.5 %pack.7 = (f32[4,64,256]{2,1,0:T(8,128)S(1)}, f32[4,64,256]{2,1,0:T(8,128)S(1)}, f32[2,64,256]{2,1,0:T(8,128)S(1)}) custom-call(s32[2]{0:T(128)S(1)} %pad_add_fusion.1.info, s32[8]{0:T(128)S(1)} %copy-done, f32[8,8,64,1024]{3,2,1,0:T(8,128)} %source.11), custom_call_target="tpu_custom_call" | custom-call | bytes 1572864 | tf_op jit(solution)/shard_map/pack/pallas_call | solution.py:117
  29.8 2.2 %collective-permute-start.8 = (f32[136,256]{1,0:T(8,128)S(1)}, f32[136,256]{1,0:T(8,128)S(1)}, u32[]{:S(2)}, u32[]{:S(2)}) collective-permute-start(f32[136,256]{1,0:T(8,128)S(1)} %select_maximum_fusion), channel_id=1, source_target_pairs={{0,8},{2,10},{4,12},{6,14},{8,0},{10,2},{12,4},{14,6},{16,24},{18,... | collective-permute-start | bytes 417800 | tf_op jit(solution)/shard_map/ppermute | solution.py:25
  32.8 2.0 %pack.8 = (f32[2,64,256]{2,1,0:T(8,128)S(1)}, f32[2,64,256]{2,1,0:T(8,128)S(1)}, f32[1,64,256]{2,1,0:T(8,128)S(1)}, f32[4,64,256]{2,1,0:T(8,128)S(1)}, f32[4,64,...) custom-call(s32[2]{0:T(128)S(1)} %pad_add_fusion.info, s32[8]{0:T(128)S(1)} %copy-done, f32[8,64,1024]{2,1,0:T(8,128)} %source.8), custom_call_target="tpu_custom_call" | custom-call | bytes 2359296 | tf_op jit(solution)/shard_map/pack/pallas_call | solution.py:117
  37.5 8.6 %collective-permute-done.9 = f32[136,256]{1,0:T(8,128)S(1)} collective-permute-done((f32[136,256]{1,0:T(8,128)S(1)}, f32[136,256]{1,0:T(8,128)S(1)}, u32[]{:S(2)}, u32[]{:S(2)}) %collective-permute-start.9) | collective-permute-done | bytes 139296 | tf_op jit(solution)/shard_map/ppermute | solution.py:25
  58.6 3.0 %collective-permute-start.18 = (f32[64,256]{1,0:T(8,128)S(1)}, f32[64,256]{1,0:T(8,128)S(1)}, u32[]{:S(2)}, u32[]{:S(2)}) collective-permute-start(f32[64,256]{1,0:T(8,128)S(1)} %fusion.53), channel_id=1, source_target_pairs={{0,8},{2,10},{4,12},{6,14},{8,0},{10,2},{12,4},{14,6},{16,24},{18,... | collective-permute-start | bytes 196616 | tf_op jit(solution)/shard_map/ppermute | solution.py:25
  61.8 2.0 %collective-permute-done.20 = f32[64,256]{1,0:T(8,128)S(1)} collective-permute-done((f32[64,256]{1,0:T(8,128)S(1)}, f32[64,256]{1,0:T(8,128)S(1)}, u32[]{:S(2)}, u32[]{:S(2)}) %collective-permute-start.20) | collective-permute-done | bytes 65568 | tf_op jit(solution)/shard_map/ppermute | solution.py:25
  68.7 3.5 %pack.9 = (f32[8,64,256]{2,1,0:T(8,128)S(1)}, f32[8,64,256]{2,1,0:T(8,128)S(1)}, f32[4,64,256]{2,1,0:T(8,128)S(1)}) custom-call(s32[2]{0:T(128)S(1)} %pad_add_fusion.1.info, s32[8]{0:T(128)S(1)} %copy-done, f32[8,8,64,1024]{3,2,1,0:T(8,128)} %source.11), custom_call_target="tpu_custom_call" | custom-call | bytes 3145728 | tf_op jit(solution)/shard_map/pack/pallas_call | solution.py:117
  73.6 2.4 %collective-permute-start.30 = (f32[64,256]{1,0:T(8,128)S(1)}, f32[64,256]{1,0:T(8,128)S(1)}, u32[]{:S(2)}, u32[]{:S(2)}) collective-permute-start(f32[64,256]{1,0:T(8,128)S(1)} %fusion.52), channel_id=1, source_target_pairs={{0,24},{2,26},{4,28},{6,30},{8,16},{10,18},{12,20},{14,22},{16,8},... | collective-permute-start | bytes 196616 | tf_op jit(solution)/shard_map/ppermute | solution.py:25
  81.0 3.7 %pack.10 = (f32[8,64,256]{2,1,0:T(8,128)S(1)}, f32[8,64,256]{2,1,0:T(8,128)S(1)}, f32[4,64,256]{2,1,0:T(8,128)S(1)}) custom-call(s32[2]{0:T(128)S(1)} %pad_add_fusion.1.info, s32[8]{0:T(128)S(1)} %copy-done, f32[8,8,64,1024]{3,2,1,0:T(8,128)} %source.11), custom_call_target="tpu_custom_call" | custom-call | bytes 3145728 | tf_op jit(solution)/shard_map/pack/pallas_call | solution.py:117
  84.7 3.5 %pack.11 = (f32[8,64,256]{2,1,0:T(8,128)S(1)}, f32[8,64,256]{2,1,0:T(8,128)S(1)}, f32[4,64,256]{2,1,0:T(8,128)S(1)}) custom-call(s32[2]{0:T(128)S(1)} %pad_add_fusion.1.info, s32[8]{0:T(128)S(1)} %copy-done, f32[8,8,64,1024]{3,2,1,0:T(8,128)} %source.11), custom_call_target="tpu_custom_call" | custom-call | bytes 3145728 | tf_op jit(solution)/shard_map/pack/pallas_call | solution.py:117
  92.4 4.8 %collective-permute-done.46.far_ref = f32[2,64,256]{2,1,0:T(8,128)S(1)} collective-permute-done((f32[2,64,256]{2,1,0:T(8,128)S(1)}, f32[2,64,256]{2,1,0:T(8,128)S(1)}, u32[]{:S(2)}, u32[]{:S(2)}) %collective-permute-start.46) | collective-permute-done | bytes 131104 | tf_op jit(solution)/shard_map/ppermute | solution.py:25
  97.8 3.3 %collective-permute-done.53.far_ref = f32[4,64,256]{2,1,0:T(8,128)S(1)} collective-permute-done((f32[4,64,256]{2,1,0:T(8,128)S(1)}, f32[4,64,256]{2,1,0:T(8,128)S(1)}, u32[]{:S(2)}, u32[]{:S(2)}) %collective-permute-start.53) | collective-permute-done | bytes 262176 | tf_op jit(solution)/shard_map/ppermute | solution.py:25
  112.7 2.0 %collective-permute-start.40 = (f32[64,256]{1,0:T(8,128)S(1)}, f32[64,256]{1,0:T(8,128)S(1)}, u32[]{:S(2)}, u32[]{:S(2)}) collective-permute-start(f32[64,256]{1,0:T(8,128)S(1)} %fusion.49), channel_id=1, source_target_pairs={{0,24},{2,26},{4,28},{6,30},{8,16},{10,18},{12,20},{14,22},{16,8},... | collective-permute-start | bytes 196616 | tf_op jit(solution)/shard_map/ppermute | solution.py:25
  117.5 2.0 %collective-permute-done.40 = f32[64,256]{1,0:T(8,128)S(1)} collective-permute-done((f32[64,256]{1,0:T(8,128)S(1)}, f32[64,256]{1,0:T(8,128)S(1)}, u32[]{:S(2)}, u32[]{:S(2)}) %collective-permute-start.40) | collective-permute-done | bytes 65568 | tf_op jit(solution)/shard_map/ppermute | solution.py:25
  130.2 7.1 %collective-permute-done.43 = f32[64,256]{1,0:T(8,128)S(1)} collective-permute-done((f32[64,256]{1,0:T(8,128)S(1)}, f32[64,256]{1,0:T(8,128)S(1)}, u32[]{:S(2)}, u32[]{:S(2)}) %collective-permute-start.43) | collective-permute-done | bytes 65568 | tf_op jit(solution)/shard_map/ppermute | solution.py:25
  137.5 1.9 collective-permute-start.50
  139.5 2.5 %collective-permute-start.48 = (f32[64,256]{1,0:T(8,128)S(1)}, f32[64,256]{1,0:T(8,128)S(1)}, u32[]{:S(2)}, u32[]{:S(2)}) collective-permute-start(f32[64,256]{1,0:T(8,128)S(1)} %fusion.45), channel_id=1, source_target_pairs={{0,8},{2,10},{4,12},{6,14},{8,0},{10,2},{12,4},{14,6},{16,24},{18,... | collective-permute-start | bytes 196616 | tf_op jit(solution)/shard_map/ppermute | solution.py:25
  153.0 2.0 %collective-permute-start.60 = (f32[64,256]{1,0:T(8,128)S(1)}, f32[64,256]{1,0:T(8,128)S(1)}, u32[]{:S(2)}, u32[]{:S(2)}) collective-permute-start(f32[64,256]{1,0:T(8,128)S(1)} %fusion.40), channel_id=1, source_target_pairs={{0,24},{2,26},{4,28},{6,30},{8,16},{10,18},{12,20},{14,22},{16,8},... | collective-permute-start | bytes 196616 | tf_op jit(solution)/shard_map/ppermute | solution.py:25
  168.9 1.9 collective-permute-start.70
  171.5 1.9 collective-permute-start.68
  184.1 2.0 %collective-permute-start.76 = (f32[64,128]{1,0:T(8,128)S(1)}, f32[64,128]{1,0:T(8,128)S(1)}, u32[]{:S(2)}, u32[]{:S(2)}) collective-permute-start(f32[64,128]{1,0:T(8,128)S(1)} %get-tuple-element.100), channel_id=1, source_target_pairs={{0,24},{2,26},{4,28},{6,30},{8,16},{10,18},{12,20},{14,22},{16,8},... | collective-permute-start | bytes 98312 | tf_op jit(solution)/shard_map/ppermute | solution.py:25
  (263 shorter events, 117.9 us)
Async XLA Ops:
  10.2 14.9 %collective-permute-start.4 = (f32[2,64,256]{2,1,0:T(8,128)S(1)}, f32[2,64,256]{2,1,0:T(8,128)S(1)}, u32[]{:S(2)}, u32[]{:S(2)}) collective-permute-start(f32[2,64,256]{2,1,0:T(8,128)S(1)} %get-tuple-element.51), channel_id=1, source_target_pairs={{0,8},{1,17},{2,10},{3,19},{4,12},{5,21},{6,14},{7,23},{8,0},{9,25... | collective-permute-start | bytes 393224 | tf_op jit(solution)/shard_map/ppermute | solution.py:170
  22.0 12.8 %collective-permute-start.11 = (f32[4,64,256]{2,1,0:T(8,128)S(1)}, f32[4,64,256]{2,1,0:T(8,128)S(1)}, u32[]{:S(2)}, u32[]{:S(2)}) collective-permute-start(f32[4,64,256]{2,1,0:T(8,128)S(1)} %get-tuple-element.57), channel_id=1, source_target_pairs={{0,2},{1,5},{2,0},{3,7},{4,6},{5,1},{6,4},{7,3},{8,10},{9,13},{10,... | collective-permute-start | bytes 786440 | tf_op jit(solution)/shard_map/ppermute | solution.py:170
  29.0 17.1 %collective-permute-start.9 = (f32[136,256]{1,0:T(8,128)S(1)}, f32[136,256]{1,0:T(8,128)S(1)}, u32[]{:S(2)}, u32[]{:S(2)}) collective-permute-start(f32[136,256]{1,0:T(8,128)S(1)} %select_maximum_fusion), channel_id=1, source_target_pairs={{0,16},{2,18},{4,20},{6,22},{8,24},{10,26},{12,28},{14,30},{16,0},... | collective-permute-start | bytes 417800 | tf_op jit(solution)/shard_map/ppermute | solution.py:25
  29.8 16.3 %collective-permute-start.8 = (f32[136,256]{1,0:T(8,128)S(1)}, f32[136,256]{1,0:T(8,128)S(1)}, u32[]{:S(2)}, u32[]{:S(2)}) collective-permute-start(f32[136,256]{1,0:T(8,128)S(1)} %select_maximum_fusion), channel_id=1, source_target_pairs={{0,8},{2,10},{4,12},{6,14},{8,0},{10,2},{12,4},{14,6},{16,24},{18,... | collective-permute-start | bytes 417800 | tf_op jit(solution)/shard_map/ppermute | solution.py:25
  32.7 14.2 %collective-permute-start.14 = (f32[2,64,256]{2,1,0:T(8,128)S(1)}, f32[2,64,256]{2,1,0:T(8,128)S(1)}, u32[]{:S(2)}, u32[]{:S(2)}) collective-permute-start(f32[2,64,256]{2,1,0:T(8,128)S(1)} %collective-permute-done.13.far_ref), channel_id=1, source_target_pairs={{0,1},{1,0},{2,3},{3,2},{4,5},{5,4},{6,7},{7,6},{8,9},{9,8},{10,11... | collective-permute-start | bytes 393224 | tf_op jit(solution)/shard_map/ppermute | solution.py:29
  34.7 17.4 %collective-permute-start.24 = (f32[2,64,256]{2,1,0:T(8,128)S(1)}, f32[2,64,256]{2,1,0:T(8,128)S(1)}, u32[]{:S(2)}, u32[]{:S(2)}) collective-permute-start(f32[2,64,256]{2,1,0:T(8,128)S(1)} %get-tuple-element.61), channel_id=1, source_target_pairs={{0,8},{1,17},{2,10},{3,19},{4,12},{5,21},{6,14},{7,23},{8,0},{9,25... | collective-permute-start | bytes 393224 | tf_op jit(solution)/shard_map/ppermute | solution.py:170
  36.1 16.0 %collective-permute-start.26 = (f32[1,64,256]{2,1,0:T(8,128)S(1)}, f32[1,64,256]{2,1,0:T(8,128)S(1)}, u32[]{:S(2)}, u32[]{:S(2)}) collective-permute-start(f32[1,64,256]{2,1,0:T(8,128)S(1)} %get-tuple-element.62), channel_id=1, source_target_pairs={{0,24},{2,26},{4,28},{6,30},{8,16},{10,18},{12,20},{14,22},{16,8},... | collective-permute-start | bytes 196616 | tf_op jit(solution)/shard_map/ppermute | solution.py:25
  52.1 20.1 %collective-permute-start.27 = (f32[1,64,256]{2,1,0:T(8,128)S(1)}, f32[1,64,256]{2,1,0:T(8,128)S(1)}, u32[]{:S(2)}, u32[]{:S(2)}) collective-permute-start(f32[1,64,256]{2,1,0:T(8,128)S(1)} %collective-permute-done.26.far_ref), channel_id=1, source_target_pairs={{0,1},{1,0},{2,3},{3,2},{4,5},{5,4},{6,7},{7,6},{8,9},{9,8},{10,11... | collective-permute-start | bytes 196616 | tf_op jit(solution)/shard_map/ppermute | solution.py:29
  52.1 20.1 %collective-permute-start.25 = (f32[2,64,256]{2,1,0:T(8,128)S(1)}, f32[2,64,256]{2,1,0:T(8,128)S(1)}, u32[]{:S(2)}, u32[]{:S(2)}) collective-permute-start(f32[2,64,256]{2,1,0:T(8,128)S(1)} %collective-permute-done.24.near_ref), channel_id=1, source_target_pairs={{0,1},{1,0},{2,3},{3,2},{4,5},{5,4},{6,7},{7,6},{8,9},{9,8},{10,11... | collective-permute-start | bytes 393224 | tf_op jit(solution)/shard_map/ppermute | solution.py:29
  72.8 19.4 %collective-permute-start.31 = (f32[8,64,256]{2,1,0:T(8,128)S(1)}, f32[8,64,256]{2,1,0:T(8,128)S(1)}, u32[]{:S(2)}, u32[]{:S(2)}) collective-permute-start(f32[8,64,256]{2,1,0:T(8,128)S(1)} %get-tuple-element.67), channel_id=1, source_target_pairs={{0,2},{1,5},{2,0},{3,7},{4,6},{5,1},{6,4},{7,3},{8,10},{9,13},{10,... | collective-permute-start | bytes 1572872 | tf_op jit(solution)/shard_map/ppermute | solution.py:170
  76.0 14.4 %collective-permute-start.33 = (f32[4,64,256]{2,1,0:T(8,128)S(1)}, f32[4,64,256]{2,1,0:T(8,128)S(1)}, u32[]{:S(2)}, u32[]{:S(2)}) collective-permute-start(f32[4,64,256]{2,1,0:T(8,128)S(1)} %get-tuple-element.68), channel_id=1, source_target_pairs={{0,6},{2,4},{4,2},{6,0},{8,14},{10,12},{12,10},{14,8},{16,22},{18,... | collective-permute-start | bytes 786440 | tf_op jit(solution)/shard_map/ppermute | solution.py:25
  77.6 12.2 %collective-permute-start.28 = (f32[64,256]{1,0:T(8,128)S(1)}, f32[64,256]{1,0:T(8,128)S(1)}, u32[]{:S(2)}, u32[]{:S(2)}) collective-permute-start(f32[64,256]{1,0:T(8,128)S(1)} %fusion.52), channel_id=1, source_target_pairs={{0,8},{2,10},{4,12},{6,14},{8,0},{10,2},{12,4},{14,6},{16,24},{18,... | collective-permute-start | bytes 196616 | tf_op jit(solution)/shard_map/ppermute | solution.py:25
  79.8 17.5 %collective-permute-start.44 = (f32[4,64,256]{2,1,0:T(8,128)S(1)}, f32[4,64,256]{2,1,0:T(8,128)S(1)}, u32[]{:S(2)}, u32[]{:S(2)}) collective-permute-start(f32[4,64,256]{2,1,0:T(8,128)S(1)} %get-tuple-element.72), channel_id=1, source_target_pairs={{0,8},{1,17},{2,10},{3,19},{4,12},{5,21},{6,14},{7,23},{8,0},{9,25... | collective-permute-start | bytes 786440 | tf_op jit(solution)/shard_map/ppermute | solution.py:170
  88.1 14.5 %collective-permute-start.51 = (f32[8,64,256]{2,1,0:T(8,128)S(1)}, f32[8,64,256]{2,1,0:T(8,128)S(1)}, u32[]{:S(2)}, u32[]{:S(2)}) collective-permute-start(f32[8,64,256]{2,1,0:T(8,128)S(1)} %get-tuple-element.78), channel_id=1, source_target_pairs={{0,2},{1,5},{2,0},{3,7},{4,6},{5,1},{6,4},{7,3},{8,10},{9,13},{10,... | collective-permute-start | bytes 1572872 | tf_op jit(solution)/shard_map/ppermute | solution.py:170
  89.9 11.3 %collective-permute-start.53 = (f32[4,64,256]{2,1,0:T(8,128)S(1)}, f32[4,64,256]{2,1,0:T(8,128)S(1)}, u32[]{:S(2)}, u32[]{:S(2)}) collective-permute-start(f32[4,64,256]{2,1,0:T(8,128)S(1)} %get-tuple-element.79), channel_id=1, source_target_pairs={{0,6},{2,4},{4,2},{6,0},{8,14},{10,12},{12,10},{14,8},{16,22},{18,... | collective-permute-start | bytes 786440 | tf_op jit(solution)/shard_map/ppermute | solution.py:25
  92.2 11.5 %collective-permute-start.32 = (f32[8,64,256]{2,1,0:T(8,128)S(1)}, f32[8,64,256]{2,1,0:T(8,128)S(1)}, u32[]{:S(2)}, u32[]{:S(2)}) collective-permute-start(f32[8,64,256]{2,1,0:T(8,128)S(1)} %collective-permute-done.31.near_ref), channel_id=1, source_target_pairs={{0,1},{1,0},{2,3},{3,2},{4,5},{5,4},{6,7},{7,6},{8,9},{9,8},{10,11... | collective-permute-start | bytes 1572872 | tf_op jit(solution)/shard_map/ppermute | solution.py:29
  102.5 23.0 %collective-permute-start.54 = (f32[4,64,256]{2,1,0:T(8,128)S(1)}, f32[4,64,256]{2,1,0:T(8,128)S(1)}, u32[]{:S(2)}, u32[]{:S(2)}) collective-permute-start(f32[4,64,256]{2,1,0:T(8,128)S(1)} %collective-permute-done.53.far_ref), channel_id=1, source_target_pairs={{0,1},{1,0},{2,3},{3,2},{4,5},{5,4},{6,7},{7,6},{8,9},{9,8},{10,11... | collective-permute-start | bytes 786440 | tf_op jit(solution)/shard_map/ppermute | solution.py:29
  102.6 23.4 %collective-permute-start.52 = (f32[8,64,256]{2,1,0:T(8,128)S(1)}, f32[8,64,256]{2,1,0:T(8,128)S(1)}, u32[]{:S(2)}, u32[]{:S(2)}) collective-permute-start(f32[8,64,256]{2,1,0:T(8,128)S(1)} %collective-permute-done.51.near_ref), channel_id=1, source_target_pairs={{0,1},{1,0},{2,3},{3,2},{4,5},{5,4},{6,7},{7,6},{8,9},{9,8},{10,11... | collective-permute-start | bytes 1572872 | tf_op jit(solution)/shard_map/ppermute | solution.py:29
  119.5 37.9 %collective-permute-start.61 = (f32[8,64,256]{2,1,0:T(8,128)S(1)}, f32[8,64,256]{2,1,0:T(8,128)S(1)}, u32[]{:S(2)}, u32[]{:S(2)}) collective-permute-start(f32[8,64,256]{2,1,0:T(8,128)S(1)} %get-tuple-element.84), channel_id=1, source_target_pairs={{0,2},{1,5},{2,0},{3,7},{4,6},{5,1},{6,4},{7,3},{8,10},{9,13},{10,... | collective-permute-start | bytes 1572872 | tf_op jit(solution)/shard_map/ppermute | solution.py:170
  122.1 20.1 %collective-permute-start.63 = (f32[4,64,256]{2,1,0:T(8,128)S(1)}, f32[4,64,256]{2,1,0:T(8,128)S(1)}, u32[]{:S(2)}, u32[]{:S(2)}) collective-permute-start(f32[4,64,256]{2,1,0:T(8,128)S(1)} %get-tuple-element.85), channel_id=1, source_target_pairs={{0,6},{2,4},{4,2},{6,0},{8,14},{10,12},{12,10},{14,8},{16,22},{18,... | collective-permute-start | bytes 786440 | tf_op jit(solution)/shard_map/ppermute | solution.py:25
  124.1 13.1 %collective-permute-start.43 = (f32[64,256]{1,0:T(8,128)S(1)}, f32[64,256]{1,0:T(8,128)S(1)}, u32[]{:S(2)}, u32[]{:S(2)}) collective-permute-start(f32[64,256]{1,0:T(8,128)S(1)} %sub.167), channel_id=1, source_target_pairs={{0,6},{2,4},{4,2},{6,0},{8,14},{10,12},{12,10},{14,8},{16,22},{18,... | collective-permute-start | bytes 196616 | tf_op jit(solution)/shard_map/ppermute | solution.py:25
  125.5 11.8 %collective-permute-start.42 = (f32[64,256]{1,0:T(8,128)S(1)}, f32[64,256]{1,0:T(8,128)S(1)}, u32[]{:S(2)}, u32[]{:S(2)}) collective-permute-start(f32[64,256]{1,0:T(8,128)S(1)} %sub.167), channel_id=1, source_target_pairs={{0,4},{2,6},{4,0},{6,2},{8,12},{10,14},{12,8},{14,10},{16,20},{18,... | collective-permute-start | bytes 196616 | tf_op jit(solution)/shard_map/ppermute | solution.py:25
  126.0 11.3 %collective-permute-start.41 = (f32[64,256]{1,0:T(8,128)S(1)}, f32[64,256]{1,0:T(8,128)S(1)}, u32[]{:S(2)}, u32[]{:S(2)}) collective-permute-start(f32[64,256]{1,0:T(8,128)S(1)} %sub.167), channel_id=1, source_target_pairs={{0,2},{2,0},{4,6},{6,4},{8,10},{10,8},{12,14},{14,12},{16,18},{18,... | collective-permute-start | bytes 196616 | tf_op jit(solution)/shard_map/ppermute | solution.py:25
  142.2 18.7 %collective-permute-start.64 = (f32[4,64,256]{2,1,0:T(8,128)S(1)}, f32[4,64,256]{2,1,0:T(8,128)S(1)}, u32[]{:S(2)}, u32[]{:S(2)}) collective-permute-start(f32[4,64,256]{2,1,0:T(8,128)S(1)} %collective-permute-done.63.far_ref), channel_id=1, source_target_pairs={{0,1},{1,0},{2,3},{3,2},{4,5},{5,4},{6,7},{7,6},{8,9},{9,8},{10,11... | collective-permute-start | bytes 786440 | tf_op jit(solution)/shard_map/ppermute | solution.py:29
  (64 other events, 438.7 us)
